TPU v7x, 256 devices: a whole 4x4x8 slice. The times are simulated.
256 devices in a mesh: lon: 16 (over z, x_hi), lat: 16 (over y, x_lo, core).
Axes of the slice: x: 4 (x_hi: 2, x_lo: 2; x = x_hi * 2 + x_lo), y: 4, z: 8, core: 2. Of those that a mesh axis runs over, the one named last changes fastest.
Arguments:
- features: bfloat16 [720, 720, 192], P('lat', 'lon'), may hold values from -6 to 6
- params: float32 [307200], P(('lon', 'lat')), may hold values from -1.5 to 1.5
- langevin_noise: float32 [307200], P(('lon', 'lat')), may hold values from -6 to 6
- upstream: bfloat16 [720, 720, 192], P('lat', 'lon'), may hold values from -6 to 6
Outputs:
- output: bfloat16 [720, 720, 192], P('lat', 'lon')
- field_grad: bfloat16 [720, 720, 192], P('lat', 'lon')
- new_params: float32 [307200], P(('lon', 'lat'))
All inputs are finite; a program needn't handle non-finite values.
Results may differ from a plain program's by a relative error of at most 0.0085.
Values may be sent and summed in bfloat16 or wider, within the bound.
A program may use at most 64 MiB of HBM per device.

v0:
```python
import math

import jax
import jax.numpy as jnp
from jax import lax
from jax.sharding import PartitionSpec as P

C = 192
H = 768
KS = 7


EPSILON = 1e-06
STEP_SIZE = 0.003
NOISE_COEF = 0.08


def padded_2(block, sides, width, periodic):
    for axis, dim in sides:
        count = lax.axis_size(axis)
        forward = [(i, i + 1) for i in range(count - 1)]
        if periodic:
            forward.append((count - 1, 0))
        backward = [(target, source) for source, target in forward]
        low = lax.ppermute(
            lax.slice_in_dim(block, block.shape[dim] - width, None, axis=dim), axis, forward
        )
        high = lax.ppermute(lax.slice_in_dim(block, 0, width, axis=dim), axis, backward)
        block = jnp.concatenate([low, block, high], axis=dim)
    return block


def unpack(weights):
    layouts = [(C, H), (H, C), (KS, KS, C), (C,), (C,), (C,), (H,), (C,), (C,)]
    pieces = []
    offset = 0
    for layout in layouts:
        length = math.prod(layout)
        pieces.append(weights[offset : offset + length].reshape(layout))
        offset = offset + length
    return pieces


def gelu_tanh(values):
    return jax.nn.gelu(values, approximate=True)


def depthwise(padded, kernel, conv_bias, lat_rows, lon_cols):
    summed = jnp.zeros((lat_rows, lon_cols, padded.shape[2]), jnp.float32) + conv_bias
    for row_off in range(KS):
        for col_off in range(KS):
            window = padded[row_off : row_off + lat_rows, col_off : col_off + lon_cols]
            summed = summed + kernel[row_off, col_off] * window.astype(jnp.float32)
    return summed


def transposed(grad_padded, kernel, lat_rows, lon_cols):
    span = KS - 1
    summed = jnp.zeros((lat_rows, lon_cols, grad_padded.shape[2]), jnp.float32)
    for row_off in range(KS):
        for col_off in range(KS):
            window = grad_padded[
                span - row_off : span - row_off + lat_rows,
                span - col_off : span - col_off + lon_cols,
            ]
            summed = summed + kernel[row_off, col_off] * window.astype(jnp.float32)
    return summed


def kernel_grad(grad_conv, padded, lat_rows, lon_cols):
    sums = []
    for row_off in range(KS):
        for col_off in range(KS):
            window = padded[row_off : row_off + lat_rows, col_off : col_off + lon_cols]
            sums.append(
                jnp.sum(grad_conv.astype(jnp.float32) * window.astype(jnp.float32), axis=(0, 1))
            )
    return jnp.stack(sums).reshape(KS, KS, -1)


def layer_pass(convolved, features, upstream, unpacked):
    w_in, w_out, kernel, conv_bias, ln_gain, ln_bias, bias_in, bias_out, layer_scale = unpacked
    mean_val = jnp.mean(convolved, axis=-1, keepdims=True)
    centred = convolved - mean_val
    inv_std = lax.rsqrt(jnp.mean(centred * centred, axis=-1, keepdims=True) + EPSILON)
    standard = centred * inv_std
    normed = (standard * ln_gain + ln_bias).astype(jnp.bfloat16)
    pre_act = jnp.einsum("ijc,ch->ijh", normed, w_in, preferred_element_type=jnp.float32) + bias_in
    activated, pullback = jax.vjp(gelu_tanh, pre_act)
    act_rounded = activated.astype(jnp.bfloat16)
    branch = (
        jnp.einsum("ijh,hc->ijc", act_rounded, w_out, preferred_element_type=jnp.float32) + bias_out
    )
    output = (features.astype(jnp.float32) + layer_scale * branch).astype(jnp.bfloat16)
    upstream_f32 = upstream.astype(jnp.float32)
    grad_branch = (layer_scale * upstream_f32).astype(jnp.bfloat16)
    grad_act = jnp.einsum("ijc,hc->ijh", grad_branch, w_out, preferred_element_type=jnp.float32)
    grad_pre = pullback(grad_act)[0].astype(jnp.bfloat16)
    grad_normed = jnp.einsum("ijh,ch->ijc", grad_pre, w_in, preferred_element_type=jnp.float32)
    scaled = grad_normed * ln_gain
    grad_conv = (
        (
            scaled
            - jnp.mean(scaled, axis=-1, keepdims=True)
            - standard * jnp.mean(scaled * standard, axis=-1, keepdims=True)
        )
        * inv_std
    ).astype(jnp.bfloat16)
    grad_in_proj = jnp.einsum("ijc,ijh->ch", normed, grad_pre, preferred_element_type=jnp.float32)
    grad_out_proj = jnp.einsum(
        "ijh,ijc->hc", act_rounded, grad_branch, preferred_element_type=jnp.float32
    )
    grad_gain = jnp.sum(grad_normed * standard, axis=(0, 1))
    grad_shift = jnp.sum(grad_normed, axis=(0, 1))
    grad_bias_in = jnp.sum(grad_pre.astype(jnp.float32), axis=(0, 1))
    grad_bias_out = jnp.sum(grad_branch.astype(jnp.float32), axis=(0, 1))
    grad_scale = jnp.sum(branch * upstream_f32, axis=(0, 1))
    layer_grads = (
        grad_in_proj,
        grad_out_proj,
        grad_gain,
        grad_shift,
        grad_bias_in,
        grad_bias_out,
        grad_scale,
    )
    return (output, grad_conv, layer_grads)


def body(features, params, langevin_noise, upstream):
    lat_rows = features.shape[0]
    lon_cols = features.shape[1]
    half_side = KS // 2
    rounded = params.astype(jnp.bfloat16)
    weights = lax.all_gather(rounded, ("lon", "lat"), axis=0, tiled=True)
    segments = unpack(weights)
    unpacked = [segments[0], segments[1]] + [
        segment.astype(jnp.float32) for segment in segments[2:]
    ]
    kernel = unpacked[2]
    conv_bias = unpacked[3]
    lon_padded = padded_2(features, (("lon", 1),), half_side, True)
    padded = padded_2(lon_padded, (("lat", 0),), half_side, False)
    convolved = depthwise(padded, kernel, conv_bias, lat_rows, lon_cols)
    output, grad_conv, layer_grads = layer_pass(convolved, features, upstream, unpacked)
    grad_kernel = kernel_grad(grad_conv, padded, lat_rows, lon_cols)
    grad_conv_bias = jnp.sum(grad_conv.astype(jnp.float32), axis=(0, 1))
    grad_lon = padded_2(grad_conv, (("lon", 1),), half_side, True)
    grad_padded = padded_2(grad_lon, (("lat", 0),), half_side, False)
    field_grad = (
        upstream.astype(jnp.float32) + transposed(grad_padded, kernel, lat_rows, lon_cols)
    ).astype(jnp.bfloat16)
    grad_in_proj, grad_out_proj, grad_gain, grad_shift, grad_bias_in, grad_bias_out, grad_scale = (
        layer_grads
    )
    flat_grads = jnp.concatenate(
        [
            grad_in_proj.reshape(-1),
            grad_out_proj.reshape(-1),
            grad_kernel.reshape(-1),
            grad_conv_bias,
            grad_gain,
            grad_shift,
            grad_bias_in,
            grad_bias_out,
            grad_scale,
        ]
    )
    full_length = params.shape[0] * lax.axis_size("lon") * lax.axis_size("lat")
    flat_grads = jnp.pad(flat_grads, (0, full_length - flat_grads.shape[0]))
    summed = lax.psum_scatter(flat_grads, ("lon", "lat"), scatter_dimension=0, tiled=True)
    new_params = params - STEP_SIZE * summed + NOISE_COEF * langevin_noise
    return (output, field_grad, new_params)


def solution(mesh):
    return jax.shard_map(
        body,
        mesh=mesh,
        in_specs=(
            P("lat", "lon", None),
            P(("lon", "lat")),
            P(("lon", "lat")),
            P("lat", "lon", None),
        ),
        out_specs=(P("lat", "lon", None), P("lat", "lon", None), P(("lon", "lat"))),
        check_vma=False,
    )
```

profile of v0, /device:TPU:1, one launch (start us, length us, event | category | flops | bytes accessed | tf_op | source)
XLA Modules:
  0.0 621.0 jit_solution(14506269792427689413)
XLA Ops:
  8.4 3.6 collective-permute-start
  12.0 5.4 collective-permute-start.1
  19.8 3.4 collective-permute-start.2
  23.2 2.1 collective-permute-start.3
  25.3 3.7 collective-permute-done.3
  29.0 2.4 maximum_maximum_fusion
  31.5 239.6 %all-reduce.6.cloned.1.call-done = bf16[307200]{0:T(1024)(128)(2,1)} async-done(((bf16[307200]{0:T(1024)(128)(2,1)}), bf16[307200]{0:T(1024)(128)(2,1)}) %all-reduce.6.cloned.1.call-update) | async-done | bytes 614416
  272.9 1.5 slice_convert_fusion.6
  274.4 20.6 %fusion.150 = (f32[45,45]{1,0:T(8,128)S(1)}, f32[45,45,192]{2,1,0:T(8,128)S(1)}) fusion(bf16[48,51,192]{2,1,0:T(8,128)(2,1)S(1)} %get-tuple-element.78, f32[192]{0:T(256)S(1)} %bitcast.120, f32[192]{0:T(256)S(1)} %bitcast.122, f32[192]{0:T(256)S(1)} %bitcast.124, f32[192]{0:T(256)S(1)} %bitcast.126, f32[192]{0:T(256)S(1)} %bitcast.128, ...), kind=kLoop, calls=%fused_computation.300 | loop fusion | flops 64538776 | bytes 35142180 | tf_op jit(solution)/shard_map/reduce_sum | solution.py:83
  300.8 4.5 multiply_convert_fusion
  305.4 6.2 convert_reduce_fusion.1
  311.6 2.3 multiply_reduce_fusion
  313.9 2.5 convolution_bitcast_fusion.1
  316.5 7.4 %fusion.133 = (f32[192]{0:T(256)S(1)}, f32[192]{0:T(256)S(1)}, f32[192]{0:T(256)S(1)}, f32[192]{0:T(256)S(1)}, f32[192]{0:T(256)S(1)}, /*index=5*/f32[192]{0:T(2...) fusion(bf16[48,51,192]{2,1,0:T(8,128)(2,1)S(1)} %get-tuple-elem, ...), kind=kLoop, calls=%fused_computation.241 | loop fusion | flops 24490944 | bytes 17931792 | tf_op jit(solution)/shard_map/reduce_sum | solution.py:76
  323.9 7.3 %fusion.105 = (f32[192]{0:T(256)}, f32[192]{0:T(256)}, f32[192]{0:T(256)}, f32[192]{0:T(256)}, f32[192]{0:T(256)}, /*index=5*/f32[192]{0:T(256)}, f32[192]{0:T(2...) fusion(bf16[45,45,192]{2,1,0:T(8,128)(2,1)S(1)} %get-tuple-elem, ...), kind=kLoop, calls=%fused_computation.213 | loop fusion | flops 21769152 | bytes 14788992 | tf_op jit(solution)/shard_map/reduce_sum | solution.py:76
  331.3 2.0 convolution_bitcast_fusion
  333.3 2.7 collective-permute-start.4
  336.0 2.4 collective-permute-start.5
  338.4 4.8 fusion.132
  343.2 2.5 fusion.59
  345.8 3.8 collective-permute-start.6
  350.0 3.3 collective-permute-start.7
  360.0 19.3 %fusion.58 = bf16[45,45,192]{2,1,0:T(8,128)(2,1)} fusion(bf16[45,45,192]{2,1,0:T(8,128)(2,1)S(1)} %copy-done.8, bf16[45,45,192]{2,1,0:T(8,128)(2,1)S(1)} %copy-done.1, bf16[45,3,192]{2,1,0:T(4,128)(2,1)S(1)} %collective-permute-done.4, bf16[45,3,192]{2,1,0:T(4,128)(2,1)S(1)} %collective-permute-done.5, bf16[48,51,192]{2,1,0:T(8,128)(2,1)S(1)} %get-tuple-element.74, ...), kind=kLoop, calls=%fused_computation.166 | loop fusion | flops 64929600 | bytes 35133312 | tf_op jit(solution)/shard_map/convert_element_type | solution.py:152
  379.3 233.5 %all-reduce.8.cloned.1.call-done = f32[307200]{0:T(1024)} async-done(((f32[307200]{0:T(1024)}), f32[307200]{0:T(1024)}) %all-reduce.8.cloned.1.call-update) | async-done | bytes 1228816
  (296 shorter events, 17.9 us)
Async XLA Ops:
  7.2 263.9 %all-reduce.6.cloned.1.call-start = ((), (), s32[]{:S(2)}) async-start(), calls=%async_computation | async-start | bytes 1228800
  8.4 11.3 %collective-permute-start = (bf16[45,3,192]{2,1,0:T(4,128)(2,1)S(1)}, bf16[45,3,192]{2,1,0:T(4,128)(2,1)S(1)}, u32[]{:S(2)}, u32[]{:S(2)}) collective-permute-start(bf16[45,3,192]{2,1,0:T(4,128)(2,1)S(1)} %get-tuple-element.83), channel_id=1, source_target_pairs={{0,16},{16,32},{32,48},{48,64},{64,80},{80,96},{96,112},{112,128},... | collective-permute-start | bytes 155528 | tf_op jit(solution)/shard_map/ppermute | solution.py:25
  12.0 7.7 %collective-permute-start.1 = (bf16[45,3,192]{2,1,0:T(4,128)(2,1)S(1)}, bf16[45,3,192]{2,1,0:T(4,128)(2,1)S(1)}, u32[]{:S(2)}, u32[]{:S(2)}) collective-permute-start(bf16[45,3,192]{2,1,0:T(4,128)(2,1)S(1)} %get-tuple-element.84), channel_id=1, source_target_pairs={{16,0},{32,16},{48,32},{64,48},{80,64},{96,80},{112,96},{128,112},... | collective-permute-start | bytes 155528 | tf_op jit(solution)/shard_map/ppermute | solution.py:28
  19.3 593.5 %all-reduce.8.cloned.1.call-start = ((), (), s32[]{:S(2)}) async-start(), calls=%async_computation.1 | async-start | bytes 2457600
  19.8 5.6 collective-permute-start.2
  23.2 5.8 collective-permute-start.3
  271.9 23.1 %copy-start.16 = (f32[1,1,192]{2,1,0:T(1,128)}, f32[1,1,192]{2,1,0:T(1,128)S(1)}, u32[]{:S(2)}) copy-start(f32[1,1,192]{2,1,0:T(1,128)S(1)} %get-tuple-element.92) | copy-start | bytes 2308
  271.9 23.1 %copy-start.18 = (f32[1,1,192]{2,1,0:T(1,128)}, f32[1,1,192]{2,1,0:T(1,128)S(1)}, u32[]{:S(2)}) copy-start(f32[1,1,192]{2,1,0:T(1,128)S(1)} %get-tuple-element.93) | copy-start | bytes 2308
  271.9 23.1 %copy-start.20 = (f32[1,1,192]{2,1,0:T(1,128)}, f32[1,1,192]{2,1,0:T(1,128)S(1)}, u32[]{:S(2)}) copy-start(f32[1,1,192]{2,1,0:T(1,128)S(1)} %get-tuple-element.94) | copy-start | bytes 2308
  271.9 23.1 %copy-start.22 = (f32[1,1,192]{2,1,0:T(1,128)}, f32[1,1,192]{2,1,0:T(1,128)S(1)}, u32[]{:S(2)}) copy-start(f32[1,1,192]{2,1,0:T(1,128)S(1)} %get-tuple-element.95) | copy-start | bytes 2308
  271.9 23.1 %copy-start.24 = (f32[1,1,192]{2,1,0:T(1,128)}, f32[1,1,192]{2,1,0:T(1,128)S(1)}, u32[]{:S(2)}) copy-start(f32[1,1,192]{2,1,0:T(1,128)S(1)} %get-tuple-element.96) | copy-start | bytes 2308
  272.0 23.1 %copy-start.26 = (f32[1,1,192]{2,1,0:T(1,128)}, f32[1,1,192]{2,1,0:T(1,128)S(1)}, u32[]{:S(2)}) copy-start(f32[1,1,192]{2,1,0:T(1,128)S(1)} %get-tuple-element.97) | copy-start | bytes 2308
  272.0 23.1 %copy-start.28 = (f32[1,1,192]{2,1,0:T(1,128)}, f32[1,1,192]{2,1,0:T(1,128)S(1)}, u32[]{:S(2)}) copy-start(f32[1,1,192]{2,1,0:T(1,128)S(1)} %get-tuple-element.98) | copy-start | bytes 2308
  272.0 23.1 %copy-start.30 = (f32[1,1,192]{2,1,0:T(1,128)}, f32[1,1,192]{2,1,0:T(1,128)S(1)}, u32[]{:S(2)}) copy-start(f32[1,1,192]{2,1,0:T(1,128)S(1)} %get-tuple-element.99) | copy-start | bytes 2308
  272.0 23.1 %copy-start.32 = (f32[1,1,192]{2,1,0:T(1,128)}, f32[1,1,192]{2,1,0:T(1,128)S(1)}, u32[]{:S(2)}) copy-start(f32[1,1,192]{2,1,0:T(1,128)S(1)} %get-tuple-element.100) | copy-start | bytes 2308
  272.0 23.1 %copy-start.34 = (f32[1,1,192]{2,1,0:T(1,128)}, f32[1,1,192]{2,1,0:T(1,128)S(1)}, u32[]{:S(2)}) copy-start(f32[1,1,192]{2,1,0:T(1,128)S(1)} %get-tuple-element.101) | copy-start | bytes 2308
  272.0 23.1 %copy-start.36 = (f32[1,1,192]{2,1,0:T(1,128)}, f32[1,1,192]{2,1,0:T(1,128)S(1)}, u32[]{:S(2)}) copy-start(f32[1,1,192]{2,1,0:T(1,128)S(1)} %get-tuple-element.102) | copy-start | bytes 2308
  323.9 29.4 %copy-start = (bf16[45,45,192]{2,1,0:T(8,128)(2,1)}, bf16[45,45,192]{2,1,0:T(8,128)(2,1)S(1)}, u32[]{:S(2)}) copy-start(bf16[45,45,192]{2,1,0:T(8,128)(2,1)S(1)} %get-tuple-element.69) | copy-start | bytes 2332804
  333.3 12.4 %collective-permute-start.4 = (bf16[45,3,192]{2,1,0:T(4,128)(2,1)S(1)}, bf16[45,3,192]{2,1,0:T(4,128)(2,1)S(1)}, u32[]{:S(2)}, u32[]{:S(2)}) collective-permute-start(bf16[45,3,192]{2,1,0:T(4,128)(2,1)S(1)} %get-tuple-element.82), channel_id=1, source_target_pairs={{0,16},{16,32},{32,48},{48,64},{64,80},{80,96},{96,112},{112,128},... | collective-permute-start | bytes 155528 | tf_op jit(solution)/shard_map/ppermute | solution.py:25
  336.0 9.7 %collective-permute-start.5 = (bf16[45,3,192]{2,1,0:T(4,128)(2,1)S(1)}, bf16[45,3,192]{2,1,0:T(4,128)(2,1)S(1)}, u32[]{:S(2)}, u32[]{:S(2)}) collective-permute-start(bf16[45,3,192]{2,1,0:T(4,128)(2,1)S(1)} %get-tuple-element.81), channel_id=1, source_target_pairs={{16,0},{32,16},{48,32},{64,48},{80,64},{96,80},{112,96},{128,112},... | collective-permute-start | bytes 155528 | tf_op jit(solution)/shard_map/ppermute | solution.py:28
  345.8 12.3 %collective-permute-start.6 = (bf16[3,51,192]{2,1,0:T(8,128)(2,1)S(1)}, bf16[3,51,192]{2,1,0:T(8,128)(2,1)S(1)}, u32[]{:S(2)}, u32[]{:S(2)}) collective-permute-start(bf16[3,51,192]{2,1,0:T(8,128)(2,1)S(1)} %get-tuple-element.75), channel_id=1, source_target_pairs={{1,0},{2,1},{3,2},{4,3},{5,4},{6,5},{7,6},{8,7},{9,8},{10,9},{11,1... | collective-permute-start | bytes 176264 | tf_op jit(solution)/shard_map/ppermute | solution.py:28
  350.0 8.2 %collective-permute-start.7 = (bf16[3,51,192]{2,1,0:T(8,128)(2,1)S(1)}, bf16[3,51,192]{2,1,0:T(8,128)(2,1)S(1)}, u32[]{:S(2)}, u32[]{:S(2)}) collective-permute-start(bf16[3,51,192]{2,1,0:T(8,128)(2,1)S(1)} %get-tuple-element.76), channel_id=1, source_target_pairs={{0,1},{1,2},{2,3},{3,4},{4,5},{5,6},{6,7},{7,8},{8,9},{9,10},{10,1... | collective-permute-start | bytes 176264 | tf_op jit(solution)/shard_map/ppermute | solution.py:25
  360.0 252.8 %copy-start.15 = (f32[1200]{0:T(1024)S(1)}, f32[1200]{0:T(1024)}, u32[]{:S(2)}) copy-start(f32[1200]{0:T(1024)} %param.5) | copy-start | bytes 14404
  360.0 252.8 %copy-start.91 = (f32[1200]{0:T(1024)S(1)}, f32[1200]{0:T(1024)}, u32[]{:S(2)}) copy-start(f32[1200]{0:T(1024)} %param.6) | copy-start | bytes 14404
  (114 other events, 915.5 us)
Sparse Core Ops, SparseCore 0:
  19.4 251.5 all-reduce.5
  357.9 254.8 all-reduce.7
where the time goes:
time: 623 us; the launch traced here: 621 us
  waiting for transfers between devices  477 us (77%)
  other arithmetic  70.7 us (11%)
  starting transfers between devices  26.8 us (4%)
  matrix products  20.1 us (3%)
  between operations  16.1 us (3%)
  local copies, waits for them, and re-layouts  10.1 us (2%)
    unnamed x4, waiting for transfers between devices  473 us
    reduce_sum x4, other arithmetic, kernel_grad(): jnp.sum(grad_conv.astype(jnp.float32) * window.astype(jnp.float32), axis=...  20.7 us
    reduce_sum x1, other arithmetic, layer_pass(): mean_val = jnp.mean(convolved, axis=-1, keepdims=True)  20.6 us
    convert_element_type x1, other arithmetic, body(): field_grad = (upstream.astype(jnp.float32) + transposed(grad_padded, kern...  19.3 us
    ppermute x4, starting transfers between devices, padded_2(): lax.ppermute(lax.slice_in_dim(block, 0, width, axis=dim), axis, backward)  13.7 us
    ppermute x4, starting transfers between devices, padded_2(): lax.ppermute(lax.slice_in_dim(block, block.shape[dim] - width, None, axis...  13.1 us
  transfers between devices with their start and end apart: 10, of which 4 were waited for; matrix products, arithmetic and copies ran while one was open for 6% of the time, Pallas kernels for 0%

commit v1 on v0

--- a/solution.py
+++ b/solution.py
@@ -1,18 +1,243 @@
-import math
+import functools
 
 import jax
 import jax.numpy as jnp
 from jax import lax
+from jax.experimental import pallas as pl
+from jax.experimental.pallas import tpu as pltpu
 from jax.sharding import PartitionSpec as P
 
 C = 192
 H = 768
 KS = 7
 
-
 EPSILON = 1e-06
 STEP_SIZE = 0.003
 NOISE_COEF = 0.08
+
+MESH = pl.DeviceIdType.MESH
+SHARD = 1200
+NLAT = 16
+NLON = 16
+GROUP_ROWS = NLAT * SHARD // 128
+SLOT = 160
+FLAT_ROWS = NLON * GROUP_ROWS
+PAD_ROWS = FLAT_ROWS + 16
+OUT_ROW = C * H // 128
+SMALL_ROW = 2 * C * H // 128
+SMALL = 58
+
+
+def first_row(k):
+    return k * SHARD // 128
+
+
+def greet(axes):
+    barrier = pltpu.get_barrier_semaphore()
+    count = 0
+    for name, size in axes:
+        me = lax.axis_index(name)
+        for d in range(1, size):
+            pl.semaphore_signal(
+                barrier, inc=1, device_id={name: lax.rem(me + d, size)}, device_id_type=MESH
+            )
+            count += 1
+    pl.semaphore_wait(barrier, count)
+
+
+def exchange(name, size, source, target, send_sem, recv_sem):
+    me = lax.axis_index(name)
+    copies = []
+    for d in range(1, size):
+        peer = lax.rem(me + d, size)
+        copy = pltpu.make_async_remote_copy(
+            src_ref=source(peer),
+            dst_ref=target(me),
+            send_sem=send_sem.at[d],
+            recv_sem=recv_sem.at[d],
+            device_id={name: peer},
+            device_id_type=MESH,
+        )
+        copy.start()
+        copies.append(copy)
+    return copies
+
+
+def lane_offset():
+    return lax.rem(lax.axis_index("lat") * (SHARD % 128), 128)
+
+
+def gather_kernel(
+    p_ref, win_ref, wout_ref, small_ref, send1, s1, group, send2, s2, flat, wide,
+    ssem1, rsem1, ssem2, rsem2,
+):
+    lat = lax.axis_index("lat")
+    lon = lax.axis_index("lon")
+    greet((("lat", NLAT), ("lon", NLON)))
+    off = lane_offset()
+    rolled = pltpu.roll(p_ref[...], off, 1)
+    above = pltpu.roll(rolled, 1, 0)
+    lane = lax.broadcasted_iota(jnp.int32, (16, 128), 1)
+    block = jnp.where(lane < off, above, rolled).astype(jnp.bfloat16)
+    send1[...] = block
+    copies = exchange("lat", NLAT, lambda peer: send1, lambda me: s1.at[me], ssem1, rsem1)
+    s1[lat] = block
+    group[...] = jnp.zeros((SLOT, 128), jnp.float32)
+    for copy in copies:
+        copy.wait()
+    for k in range(NLAT):
+        rows = pl.ds(first_row(k), 16)
+        group[rows, :] = group[rows, :] + s1[k].astype(jnp.float32)
+    packed = group[...].astype(jnp.bfloat16)
+    send2[...] = packed
+    copies = exchange("lon", NLON, lambda peer: send2, lambda me: s2.at[me], ssem2, rsem2)
+    s2[lon] = packed
+    for copy in copies:
+        copy.wait()
+    for k in range(NLON):
+        flat[pl.ds(k * GROUP_ROWS, SLOT), :] = s2[k].astype(jnp.float32)
+    for j in range(H // 128):
+        win_ref[:, pl.ds(128 * j, 128)] = flat[pl.ds(j, C, stride=H // 128), :].astype(jnp.bfloat16)
+    unpack_rows(flat, OUT_ROW, H // 2, wide)
+    wout_ref[...] = wide[...].astype(jnp.bfloat16)
+    unpack_rows(flat, SMALL_ROW, SMALL // 2, small_ref)
+
+
+def unpack_rows(flat, base, pairs, out):
+    first = flat[pl.ds(base, pairs, stride=3), :]
+    middle = flat[pl.ds(base + 1, pairs, stride=3), :]
+    last = flat[pl.ds(base + 2, pairs, stride=3), :]
+    low = lax.broadcasted_iota(jnp.int32, (pairs, 128), 1) < 64
+    middle_turned = pltpu.roll(middle, 64, 1)
+    last_turned = pltpu.roll(last, 64, 1)
+    out[0, 0:pairs, :] = first
+    out[0, pairs : 2 * pairs, :] = jnp.where(low, middle_turned, last_turned)
+    out[1, 0:pairs, :] = middle
+    out[1, pairs : 2 * pairs, :] = last_turned
+
+
+def pack_rows(flat, base, pairs, values):
+    low = lax.broadcasted_iota(jnp.int32, (pairs, 128), 1) < 64
+    odd_turned = pltpu.roll(values[0, pairs : 2 * pairs, :], 64, 1)
+    odd_tail_turned = pltpu.roll(values[1, pairs : 2 * pairs, :], 64, 1)
+    flat[pl.ds(base, pairs, stride=3), :] = values[0, 0:pairs, :]
+    flat[pl.ds(base + 1, pairs, stride=3), :] = jnp.where(low, values[1, 0:pairs, :], odd_turned)
+    flat[pl.ds(base + 2, pairs, stride=3), :] = jnp.where(low, odd_turned, odd_tail_turned)
+
+
+def reduce_kernel(
+    gin_ref, gout_ref, small_ref, p_ref, noise_ref, new_ref, flat, send1, r1, group, send2, r2,
+    ssem1, rsem1, ssem2, rsem2,
+):
+    lat = lax.axis_index("lat")
+    lon = lax.axis_index("lon")
+    greet((("lat", NLAT), ("lon", NLON)))
+    flat[pl.ds(SMALL_ROW + 80, PAD_ROWS - SMALL_ROW - 80), :] = jnp.zeros(
+        (PAD_ROWS - SMALL_ROW - 80, 128), jnp.float32
+    )
+    for j in range(H // 128):
+        flat[pl.ds(j, C, stride=H // 128), :] = gin_ref[:, pl.ds(128 * j, 128)]
+    pack_rows(flat, OUT_ROW, H // 2, gout_ref)
+    pack_rows(flat, SMALL_ROW, SMALL // 2, small_ref)
+    for k in range(NLON):
+        send1[k] = flat[pl.ds(k * GROUP_ROWS, SLOT), :].astype(jnp.bfloat16)
+    copies = exchange("lon", NLON, lambda peer: send1.at[peer], lambda me: r1.at[me], ssem1, rsem1)
+    r1[lon] = send1[lon]
+    for copy in copies:
+        copy.wait()
+    total = r1[0].astype(jnp.float32)
+    for k in range(1, NLON):
+        total = total + r1[k].astype(jnp.float32)
+    group[...] = total
+    for k in range(NLAT):
+        send2[k] = group[pl.ds(first_row(k), 16), :]
+    copies = exchange("lat", NLAT, lambda peer: send2.at[peer], lambda me: r2.at[me], ssem2, rsem2)
+    r2[lat] = send2[lat]
+    for copy in copies:
+        copy.wait()
+    total = r2[0]
+    for k in range(1, NLAT):
+        total = total + r2[k]
+    off = lane_offset()
+    lane = lax.broadcasted_iota(jnp.int32, (16, 128), 1)
+    below = pltpu.roll(total, 15, 0)
+    mixed = jnp.where(lane < off, below, total)
+    grads = pltpu.roll(mixed, lax.rem(128 - off, 128), 1)
+    new_ref[...] = p_ref[...] - STEP_SIZE * grads + NOISE_COEF * noise_ref[...]
+
+
+VM = pl.BlockSpec(memory_space=pltpu.VMEM)
+
+
+def comm_params(number):
+    return pltpu.CompilerParams(
+        collective_id=number, has_side_effects=True, vmem_limit_bytes=48 * 1024 * 1024
+    )
+
+
+def dma(n):
+    return pltpu.SemaphoreType.DMA((n,))
+
+
+def gather_weights(params):
+    padded = jnp.pad(params, (0, 2048 - SHARD)).reshape(16, 128)
+    return pl.pallas_call(
+        gather_kernel,
+        out_shape=(
+            jax.ShapeDtypeStruct((C, H), jnp.bfloat16),
+            jax.ShapeDtypeStruct((2, H, 128), jnp.bfloat16),
+            jax.ShapeDtypeStruct((2, SMALL, 128), jnp.float32),
+        ),
+        in_specs=[VM],
+        out_specs=(VM, VM, VM),
+        scratch_shapes=[
+            pltpu.VMEM((16, 128), jnp.bfloat16),
+            pltpu.VMEM((NLAT, 16, 128), jnp.bfloat16),
+            pltpu.VMEM((SLOT, 128), jnp.float32),
+            pltpu.VMEM((SLOT, 128), jnp.bfloat16),
+            pltpu.VMEM((NLON, SLOT, 128), jnp.bfloat16),
+            pltpu.VMEM((PAD_ROWS, 128), jnp.float32),
+            pltpu.VMEM((2, H, 128), jnp.float32),
+            dma(NLAT), dma(NLAT), dma(NLON), dma(NLON),
+        ],
+        compiler_params=comm_params(0),
+        name="gather_weights",
+    )(padded)
+
+
+def reduce_step(grad_in, grad_out, small, params, noise):
+    padded = jnp.pad(params, (0, 2048 - SHARD)).reshape(16, 128)
+    padded_noise = jnp.pad(noise, (0, 2048 - SHARD)).reshape(16, 128)
+    out = pl.pallas_call(
+        reduce_kernel,
+        out_shape=jax.ShapeDtypeStruct((16, 128), jnp.float32),
+        in_specs=[VM] * 5,
+        out_specs=VM,
+        scratch_shapes=[
+            pltpu.VMEM((PAD_ROWS, 128), jnp.float32),
+            pltpu.VMEM((NLON, SLOT, 128), jnp.bfloat16),
+            pltpu.VMEM((NLON, SLOT, 128), jnp.bfloat16),
+            pltpu.VMEM((SLOT, 128), jnp.float32),
+            pltpu.VMEM((NLAT, 16, 128), jnp.float32),
+            pltpu.VMEM((NLAT, 16, 128), jnp.float32),
+            dma(NLON), dma(NLON), dma(NLAT), dma(NLAT),
+        ],
+        compiler_params=comm_params(1),
+        name="reduce_step",
+    )(grad_in, grad_out, small, padded, padded_noise)
+    return out.reshape(2048)[:SHARD]
+
+
+def join_rows(halves):
+    pairs = halves.shape[1] // 2
+    rows = jnp.concatenate([halves[0], halves[1, :, :64]], axis=1)
+    return rows.reshape(2, pairs, C).transpose(1, 0, 2).reshape(2 * pairs, C)
+
+
+def split_rows(rows):
+    pairs = rows.shape[0] // 2
+    ordered = rows.reshape(pairs, 2, C).transpose(1, 0, 2).reshape(2 * pairs, C)
+    return jnp.stack([ordered[:, :128], jnp.pad(ordered[:, 128:], ((0, 0), (0, 64)))])
 
 
 def padded_2(block, sides, width, periodic):
@@ -30,17 +255,6 @@
     return block
 
 
-def unpack(weights):
-    layouts = [(C, H), (H, C), (KS, KS, C), (C,), (C,), (C,), (H,), (C,), (C,)]
-    pieces = []
-    offset = 0
-    for layout in layouts:
-        length = math.prod(layout)
-        pieces.append(weights[offset : offset + length].reshape(layout))
-        offset = offset + length
-    return pieces
-
-
 def gelu_tanh(values):
     return jax.nn.gelu(values, approximate=True)
 
@@ -75,11 +289,11 @@
             sums.append(
                 jnp.sum(grad_conv.astype(jnp.float32) * window.astype(jnp.float32), axis=(0, 1))
             )
-    return jnp.stack(sums).reshape(KS, KS, -1)
+    return jnp.stack(sums)
 
 
 def layer_pass(convolved, features, upstream, unpacked):
-    w_in, w_out, kernel, conv_bias, ln_gain, ln_bias, bias_in, bias_out, layer_scale = unpacked
+    w_in, w_out, ln_gain, ln_bias, bias_in, bias_out, layer_scale = unpacked
     mean_val = jnp.mean(convolved, axis=-1, keepdims=True)
     centred = convolved - mean_val
     inv_std = lax.rsqrt(jnp.mean(centred * centred, axis=-1, keepdims=True) + EPSILON)
@@ -131,18 +345,19 @@
     lat_rows = features.shape[0]
     lon_cols = features.shape[1]
     half_side = KS // 2
-    rounded = params.astype(jnp.bfloat16)
-    weights = lax.all_gather(rounded, ("lon", "lat"), axis=0, tiled=True)
-    segments = unpack(weights)
-    unpacked = [segments[0], segments[1]] + [
-        segment.astype(jnp.float32) for segment in segments[2:]
-    ]
-    kernel = unpacked[2]
-    conv_bias = unpacked[3]
+    w_in, w_out_halves, small_halves = gather_weights(params)
+    w_out = join_rows(w_out_halves)
+    small = join_rows(small_halves)
+    kernel = small[: KS * KS].reshape(KS, KS, C)
+    conv_bias, ln_gain, ln_bias = small[49], small[50], small[51]
+    bias_in = small[52:56].reshape(H)
+    bias_out, layer_scale = small[56], small[57]
     lon_padded = padded_2(features, (("lon", 1),), half_side, True)
     padded = padded_2(lon_padded, (("lat", 0),), half_side, False)
     convolved = depthwise(padded, kernel, conv_bias, lat_rows, lon_cols)
-    output, grad_conv, layer_grads = layer_pass(convolved, features, upstream, unpacked)
+    output, grad_conv, layer_grads = layer_pass(
+        convolved, features, upstream, (w_in, w_out, ln_gain, ln_bias, bias_in, bias_out, layer_scale)
+    )
     grad_kernel = kernel_grad(grad_conv, padded, lat_rows, lon_cols)
     grad_conv_bias = jnp.sum(grad_conv.astype(jnp.float32), axis=(0, 1))
     grad_lon = padded_2(grad_conv, (("lon", 1),), half_side, True)
@@ -153,23 +368,20 @@
     grad_in_proj, grad_out_proj, grad_gain, grad_shift, grad_bias_in, grad_bias_out, grad_scale = (
         layer_grads
     )
-    flat_grads = jnp.concatenate(
+    small_grads = jnp.concatenate(
         [
-            grad_in_proj.reshape(-1),
-            grad_out_proj.reshape(-1),
-            grad_kernel.reshape(-1),
-            grad_conv_bias,
-            grad_gain,
-            grad_shift,
-            grad_bias_in,
-            grad_bias_out,
-            grad_scale,
+            grad_kernel,
+            grad_conv_bias[None],
+            grad_gain[None],
+            grad_shift[None],
+            grad_bias_in.reshape(4, C),
+            grad_bias_out[None],
+            grad_scale[None],
         ]
     )
-    full_length = params.shape[0] * lax.axis_size("lon") * lax.axis_size("lat")
-    flat_grads = jnp.pad(flat_grads, (0, full_length - flat_grads.shape[0]))
-    summed = lax.psum_scatter(flat_grads, ("lon", "lat"), scatter_dimension=0, tiled=True)
-    new_params = params - STEP_SIZE * summed + NOISE_COEF * langevin_noise
+    new_params = reduce_step(
+        grad_in_proj, split_rows(grad_out_proj), split_rows(small_grads), params, langevin_noise
+    )
     return (output, field_grad, new_params)
 
 

time: 623 us -> 187 us (0.30)
  waiting for transfers between devices: 477 us -> 6.35 us
  Pallas kernels: 0 us -> 56.3 us
  between operations: 16.1 us -> 2.47 us
  other arithmetic: 70.7 us -> 63.1 us
    unnamed x4 -> x0, waiting for transfers between devices: 473 us -> none
    pallas_call x0 -> x2, Pallas kernels: none -> 56.3 us  [the longest x1 29.5 us: gather_weights(): pl.pallas_call(gather_kernel, out_shape=(jax.ShapeDtypeStruct((C, H), jnp...]
  transfers between devices with their start and end apart: 10 -> 8, of which waited for: 4 -> 3; matrix products, arithmetic and copies ran while one was open for 6% -> 2% of each run, Pallas kernels for 0% -> 30%
where the time goes in v1:
time: 187 us; the launch traced here: 186 us
  other arithmetic  63.1 us (34%)
  Pallas kernels  56.3 us (30%)
  starting transfers between devices  25.6 us (14%)
  matrix products  24.8 us (13%)
  local copies, waits for them, and re-layouts  7.88 us (4%)
  waiting for transfers between devices  6.35 us (3%)
  between operations  2.47 us (1%)
    pallas_call x1, Pallas kernels, gather_weights(): pl.pallas_call(gather_kernel, out_shape=(jax.ShapeDtypeStruct((C, H), jnp...  29.5 us
    pallas_call x1, Pallas kernels, reduce_step(): pl.pallas_call(reduce_kernel, out_shape=jax.ShapeDtypeStruct((16, 128), j...  26.9 us
    reduce_sum x4, other arithmetic, kernel_grad(): jnp.sum(grad_conv.astype(jnp.float32) * window.astype(jnp.float32), axis=...  20.1 us
    convert_element_type x1, other arithmetic, body(): field_grad = (upstream.astype(jnp.float32) + transposed(grad_padded, kern...  19.3 us
    reduce_sum x1, other arithmetic, layer_pass(): mean_val = jnp.mean(convolved, axis=-1, keepdims=True)  18.2 us
    ppermute x4, starting transfers between devices, padded_2(): lax.ppermute(lax.slice_in_dim(block, block.shape[dim] - width, None, axis...  13.2 us
    ppermute x4, starting transfers between devices, padded_2(): lax.ppermute(lax.slice_in_dim(block, 0, width, axis=dim), axis, backward)  12.3 us
    dot_general x1, matrix products, layer_pass(): jnp.einsum('ijc,hc->ijh', grad_branch, w_out, preferred_element_type=jnp....  6.28 us
  transfers between devices with their start and end apart: 8, of which 3 were waited for; matrix products, arithmetic and copies ran while one was open for 2% of the time, Pallas kernels for 30%

profile of v1, /device:TPU:1, one launch (start us, length us, event | category | flops | bytes accessed | tf_op | source)
XLA Modules:
  0.0 186.4 jit_solution(9737029919537820891)
XLA Ops:
  1.8 3.6 %collective-permute-start = (bf16[45,3,192]{2,1,0:T(4,128)(2,1)S(1)}, bf16[45,3,192]{2,1,0:T(4,128)(2,1)S(1)}, u32[]{:S(2)}, u32[]{:S(2)}) collective-permute-start(bf16[45,3,192]{2,1,0:T(4,128)(2,1)S(1)} %get-tuple-element.89), channel_id=1, source_target_pairs={{0,16},{16,32},{32,48},{48,64},{64,80},{80,96},{96,112},{112,128},... | collective-permute-start | bytes 155528 | tf_op jit(solution)/shard_map/ppermute | solution.py:250
  5.5 5.4 %collective-permute-start.1 = (bf16[45,3,192]{2,1,0:T(4,128)(2,1)S(1)}, bf16[45,3,192]{2,1,0:T(4,128)(2,1)S(1)}, u32[]{:S(2)}, u32[]{:S(2)}) collective-permute-start(bf16[45,3,192]{2,1,0:T(4,128)(2,1)S(1)} %get-tuple-element.90), channel_id=1, source_target_pairs={{16,0},{32,16},{48,32},{64,48},{80,64},{96,80},{112,96},{128,112},... | collective-permute-start | bytes 155528 | tf_op jit(solution)/shard_map/ppermute | solution.py:253
  11.5 29.5 %gather_weights.1 = (bf16[192,768]{1,0:T(8,128)(2,1)S(1)}, bf16[2,768,128]{2,1,0:T(8,128)(2,1)S(1)}, f32[2,58,128]{2,1,0:T(8,128)S(1)}) custom-call(f32[16,128]{1,0:T(8,128)S(1)} %pad_bitcast_fusion.3.p_ref), custom_call_target="tpu_custom_call" | custom-call | tf_op jit(solution)/shard_map/gather_weights/pallas_call | solution.py:184
  44.4 2.2 %collective-permute-start.2 = (bf16[3,51,192]{2,1,0:T(8,128)(2,1)S(1)}, bf16[3,51,192]{2,1,0:T(8,128)(2,1)S(1)}, u32[]{:S(2)}, u32[]{:S(2)}) collective-permute-start(bf16[3,51,192]{2,1,0:T(8,128)(2,1)S(1)} %get-tuple-element.85), channel_id=1, source_target_pairs={{0,1},{1,2},{2,3},{3,4},{4,5},{5,6},{6,7},{7,8},{8,9},{9,10},{10,1... | collective-permute-start | bytes 176264 | tf_op jit(solution)/shard_map/ppermute | solution.py:250
  46.6 2.4 %collective-permute-start.3 = (bf16[3,51,192]{2,1,0:T(8,128)(2,1)S(1)}, bf16[3,51,192]{2,1,0:T(8,128)(2,1)S(1)}, u32[]{:S(2)}, u32[]{:S(2)}) collective-permute-start(bf16[3,51,192]{2,1,0:T(8,128)(2,1)S(1)} %get-tuple-element.86), channel_id=1, source_target_pairs={{1,0},{2,1},{3,2},{4,3},{5,4},{6,5},{7,6},{8,7},{9,8},{10,9},{11,1... | collective-permute-start | bytes 176264 | tf_op jit(solution)/shard_map/ppermute | solution.py:253
  49.1 3.5 %collective-permute-done.3 = bf16[3,51,192]{2,1,0:T(8,128)(2,1)S(1)} collective-permute-done((bf16[3,51,192]{2,1,0:T(8,128)(2,1)S(1)}, bf16[3,51,192]{2,1,0:T(8,128)(2,1)S(1)}, u32[]{:S(2)}, u32[]{:S(2)}) %collective-permute-start.3) | collective-permute-done | bytes 58784 | tf_op jit(solution)/shard_map/ppermute | solution.py:253
  52.6 2.5 %maximum_maximum_fusion = (bf16[48,51,192]{2,1,0:T(8,128)(2,1)S(1)}, bf16[48,51,192]{2,1,0:T(8,128)(2,1)S(1)}) fusion(bf16[45,3,192]{2,1,0:T(4,128)(2,1)S(1)} %collective-permute-done.1, bf16[45,45,192]{2,1,0:T(8,128)(2,1)} %param.4, bf16[45,3,192]{2,1,0:T(4,128)(2,1)S(1)} %collective-permute-done, bf16[3,51,192]{2,1,0:T(8,128)(2,1)S(1)} %collective-permute-done.2, ...), kind=kLoop, calls=%fused_computation.258 | loop fusion | flops 7520256 | bytes 2878848 | tf_op jit(solution)/shard_map/concatenate | solution.py:254
  55.5 18.2 %fusion.151 = (f32[45,45]{1,0:T(8,128)S(1)}, f32[45,45,192]{2,1,0:T(8,128)S(1)}) fusion(bf16[48,51,192]{2,1,0:T(8,128)(2,1)S(1)} %get-tuple-element.84, f32[192]{0:T(256)S(1)} %bitcast.205, f32[192]{0:T(256)S(1)} %bitcast.207, f32[192]{0:T(256)S(1)} %bitcast.209, f32[192]{0:T(256)S(1)} %bitcast.211, f32[192]{0:T(256)S(1)} %bitcast.213, ...), kind=kLoop, calls=%fused_computation.303 | loop fusion | flops 64538776 | bytes 35142180 | tf_op jit(solution)/shard_map/reduce_sum | solution.py:297
  74.5 5.0 %multiply_convert_fusion = (bf16[45,45,768]{2,1,0:T(8,128)(2,1)}, f32[45,45,768]{2,1,0:T(8,128)S(1)}) fusion(f32[768]{0:T(1024)S(1)} %add.416, bf16[192,768]{1,0:T(8,128)(2,1)S(1)} %get-tuple-element.7, f32[45,45,192]{2,1,0:T(8,128)S(1)} %get-tuple-element.77, f32[192]{0:T(256)} %bitcast.54, f32[192]{0:T(256)} %bitcast.53, f32[45,45]{1,0:T(8,128)S(1)} %add_rsqrt_fusion, ...), kind=kOutput, calls=%fused_computation.61 | convolution fusion | flops 614692800 | bytes 11202120 | tf_op jit(solution)/shard_map/ijc,ch->ijh/dot_general | solution.py:302
  79.5 6.3 %convert_reduce_fusion.1 = (f32[768]{0:T(1024)S(1)}, bf16[45,45,768]{2,1,0:T(8,128)(2,1)S(1)}) fusion(f32[45,45,768]{2,1,0:T(8,128)S(1)} %get-tuple-element.146, f32[768]{0:T(1024)S(1)} %add.416, bf16[768,192]{1,0:T(8,128)(2,1)S(1)} %reshape.81, bf16[45,45,192]{2,1,0:T(8,128)(2,1)S(1)} %copy-done.5, f32[192]{0:T(256)} %bitcast.2), kind=kOutput, calls=%fused_computation.60 | convolution fusion | flops 634132032 | bytes 10410624 | tf_op jit(solution)/shard_map/ijc,hc->ijh/dot_general | solution.py:311
  85.8 2.5 %multiply_reduce_fusion = (f32[192]{0:T(256)S(1)}, f32[45,45]{1,0:T(8,128)S(1)}, f32[45,45]{1,0:T(8,128)S(1)}, f32[192]{0:T(256)S(1)}, f32[45,45,192]{2,1,0:T(8,128)S(1)}) fusion(f32[45,45,192]{2,1,0:T(8,128)S(1)} %get-tuple-element.77, f32[45,45]{1,0:T(8,128)S(1)} %add_rsqrt_fusion, f32[45,45]{1,0:T(8,128)S(1)} %broadcast_multiply_fusion.2, ...), kind=kOutput, calls=%fused_computation.243 | convolution fusion | flops 600691520 | bytes 6550416 | tf_op jit(solution)/shard_map/ijh,ch->ijc/dot_general | solution.py:313
  88.4 8.1 %fusion.133 = (f32[192]{0:T(256)S(1)}, f32[192]{0:T(256)S(1)}, f32[192]{0:T(256)S(1)}, f32[192]{0:T(256)S(1)}, f32[192]{0:T(256)S(1)}, /*index=5*/f32[192]{0:T(2...) fusion(bf16[48,51,192]{2,1,0:T(8,128)(2,1)S(1)} %get-tuple-elem, ...), kind=kLoop, calls=%fused_computation.241 | loop fusion | flops 24490944 | bytes 17931792 | tf_op jit(solution)/shard_map/reduce_sum | solution.py:290
  96.5 6.6 %fusion.105 = (f32[192]{0:T(256)S(1)}, f32[192]{0:T(256)S(1)}, f32[192]{0:T(256)S(1)}, f32[192]{0:T(256)S(1)}, f32[192]{0:T(256)S(1)}, /*index=5*/f32[192]{0:T(2...) fusion(bf16[45,45,192]{2,1,0:T(8,128)(2,1)S(1)} %get-tuple-elem, ...), kind=kLoop, calls=%fused_computation.213 | loop fusion | flops 21769152 | bytes 14788992 | tf_op jit(solution)/shard_map/reduce_sum | solution.py:290
  104.4 5.1 %fusion.59 = (f32[192]{0:T(256)S(1)}, f32[192]{0:T(256)S(1)}, bf16[45,45,192]{2,1,0:T(8,128)(2,1)}) fusion(bf16[45,45,192]{2,1,0:T(8,128)(2,1)} %param.7, f32[192]{0:T(256)S(1)} %bitcast.298, f32[192]{0:T(256)} %bitcast.2, bf16[45,45,192]{2,1,0:T(8,128)(2,1)} %param.4, bf16[45,45,768]{2,1,0:T(8,128)(2,1)} %get-tuple-element.145, ...), kind=kOutput, calls=%fused_computation.167 | convolution fusion | flops 601862016 | bytes 5741184 | tf_op jit(solution)/shard_map/ijh,hc->ijc/dot_general | solution.py:306
  109.5 4.2 %fusion.132 = (f32[192]{0:T(256)S(1)}, f32[192]{0:T(256)S(1)}, f32[192]{0:T(256)S(1)}, f32[192]{0:T(256)S(1)}, f32[192]{0:T(256)S(1)}, /*index=5*/f32[192]{0:T(2...) fusion(bf16[45,45,192]{2,1,0:T(8,128)(2,1)S(1)} %get-tuple-element.75, ...), kind=kLoop, calls=%fused_computation.240 | loop fusion | flops 19049280 | bytes 3999360 | tf_op jit(solution)/shard_map/reduce_sum | solution.py:290
  114.0 3.5 %convolution_bitcast_fusion = f32[768,192]{1,0:T(8,128)S(1)} fusion(bf16[45,45,768]{2,1,0:T(8,128)(2,1)} %get-tuple-element.145, bf16[45,45,192]{2,1,0:T(8,128)(2,1)} %param.7, f32[192]{0:T(256)} %bitcast.2), kind=kOutput, calls=%fused_computation.262 | convolution fusion | flops 598363200 | bytes 4478592 | tf_op jit(solution)/shard_map/ijh,ijc->hc/dot_general | solution.py:324
  117.9 2.3 %convolution_bitcast_fusion.1.gin_ref = f32[192,768]{1,0:T(8,128)S(1)} fusion(bf16[45,45,768]{2,1,0:T(8,128)(2,1)S(1)} %copy-done.90, f32[45,45,192]{2,1,0:T(8,128)S(1)} %copy-done.1, f32[192]{0:T(256)} %bitcast.54, f32[192]{0:T(256)} %bitcast.53, f32[45,45]{1,0:T(8,128)S(1)} %add_rsqrt_fusion, f32[45,45]{1,0:T(8,128)S(1)} %broadcast_multiply_fusion.2), kind=kOutput, calls=%fused_computation.263 | convolution fusion | flops 599140800 | bytes 5273160 | tf_op jit(solution)/shard_map/ijc,ijh->ch/dot_general | solution.py:323
  122.3 2.4 %collective-permute-start.4 = (bf16[45,3,192]{2,1,0:T(4,128)(2,1)S(1)}, bf16[45,3,192]{2,1,0:T(4,128)(2,1)S(1)}, u32[]{:S(2)}, u32[]{:S(2)}) collective-permute-start(bf16[45,3,192]{2,1,0:T(4,128)(2,1)S(1)} %copy-done.9), channel_id=1, source_target_pairs={{0,16},{16,32},{32,48},{48,64},{64,80},{80,96},{96,112},{112,128},... | collective-permute-start | bytes 155528 | tf_op jit(solution)/shard_map/ppermute | solution.py:250
  124.8 2.6 %collective-permute-start.5 = (bf16[45,3,192]{2,1,0:T(4,128)(2,1)S(1)}, bf16[45,3,192]{2,1,0:T(4,128)(2,1)S(1)}, u32[]{:S(2)}, u32[]{:S(2)}) collective-permute-start(bf16[45,3,192]{2,1,0:T(4,128)(2,1)S(1)} %copy-done.8), channel_id=1, source_target_pairs={{16,0},{32,16},{48,32},{64,48},{80,64},{96,80},{112,96},{128,112},... | collective-permute-start | bytes 155528 | tf_op jit(solution)/shard_map/ppermute | solution.py:253
  127.5 1.9 %collective-permute-done.4 = bf16[45,3,192]{2,1,0:T(4,128)(2,1)S(1)} collective-permute-done((bf16[45,3,192]{2,1,0:T(4,128)(2,1)S(1)}, bf16[45,3,192]{2,1,0:T(4,128)(2,1)S(1)}, u32[]{:S(2)}, u32[]{:S(2)}) %collective-permute-start.4) | collective-permute-done | bytes 51872 | tf_op jit(solution)/shard_map/ppermute | solution.py:250
  130.4 1.9 %collective-permute-start.6 = (bf16[3,51,192]{2,1,0:T(8,128)(2,1)S(1)}, bf16[3,51,192]{2,1,0:T(8,128)(2,1)S(1)}, u32[]{:S(2)}, u32[]{:S(2)}) collective-permute-start(bf16[3,51,192]{2,1,0:T(8,128)(2,1)S(1)} %get-tuple-element.81), channel_id=1, source_target_pairs={{1,0},{2,1},{3,2},{4,3},{5,4},{6,5},{7,6},{8,7},{9,8},{10,9},{11,1... | collective-permute-start | bytes 176264 | tf_op jit(solution)/shard_map/ppermute | solution.py:253
  132.3 4.9 %collective-permute-start.7 = (bf16[3,51,192]{2,1,0:T(8,128)(2,1)S(1)}, bf16[3,51,192]{2,1,0:T(8,128)(2,1)S(1)}, u32[]{:S(2)}, u32[]{:S(2)}) collective-permute-start(bf16[3,51,192]{2,1,0:T(8,128)(2,1)S(1)} %get-tuple-element.82), channel_id=1, source_target_pairs={{0,1},{1,2},{2,3},{3,4},{4,5},{5,6},{6,7},{7,8},{8,9},{9,10},{10,1... | collective-permute-start | bytes 176264 | tf_op jit(solution)/shard_map/ppermute | solution.py:250
  137.3 26.9 %reduce_step.1 = f32[16,128]{1,0:T(8,128)S(1)} custom-call(f32[192,768]{1,0:T(8,128)S(1)} %convolution_bitcast_fusion.1.gin_ref, f32[2,768,128]{2,1,0:T(8,128)S(1)} %pad_maximum_fusion.6.gout_ref, f32[2,58,128]{2,1,0:T(8,128)S(1)} %pad_maximum_fusion.13.small_ref, f32[16,128]{1,0:T(8,128)S(1)} %pad_bitcast_fusion.3.p_ref, ...), custom_call_target="tpu_custom_call" | custom-call | tf_op jit(solution)/shard_map/reduce_step/pallas_call | solution.py:211
  166.5 19.3 %fusion.58 = bf16[45,45,192]{2,1,0:T(8,128)(2,1)} fusion(bf16[45,45,192]{2,1,0:T(8,128)(2,1)S(1)} %copy-done.6, bf16[45,45,192]{2,1,0:T(8,128)(2,1)S(1)} %get-tuple-element.75, bf16[45,3,192]{2,1,0:T(4,128)(2,1)S(1)} %collective-permute-done.4, bf16[45,3,192]{2,1,0:T(4,128)(2,1)S(1)} %collective-permute-done.5, ...), kind=kLoop, calls=%fused_computation.166 | loop fusion | flops 64929600 | bytes 35133312 | tf_op jit(solution)/shard_map/convert_element_type | solution.py:367
  (238 shorter events, 12.9 us)
Async XLA Ops:
  0.6 43.7 %copy-start.2 = (bf16[45,45,192]{2,1,0:T(8,128)(2,1)S(1)}, bf16[45,45,192]{2,1,0:T(8,128)(2,1)}, u32[]{:S(2)}) copy-start(bf16[45,45,192]{2,1,0:T(8,128)(2,1)} %param.4) | copy-start | bytes 2332804
  1.8 42.4 %collective-permute-start = (bf16[45,3,192]{2,1,0:T(4,128)(2,1)S(1)}, bf16[45,3,192]{2,1,0:T(4,128)(2,1)S(1)}, u32[]{:S(2)}, u32[]{:S(2)}) collective-permute-start(bf16[45,3,192]{2,1,0:T(4,128)(2,1)S(1)} %get-tuple-element.89), channel_id=1, source_target_pairs={{0,16},{16,32},{32,48},{48,64},{64,80},{80,96},{96,112},{112,128},... | collective-permute-start | bytes 155528 | tf_op jit(solution)/shard_map/ppermute | solution.py:250
  5.5 38.8 %collective-permute-start.1 = (bf16[45,3,192]{2,1,0:T(4,128)(2,1)S(1)}, bf16[45,3,192]{2,1,0:T(4,128)(2,1)S(1)}, u32[]{:S(2)}, u32[]{:S(2)}) collective-permute-start(bf16[45,3,192]{2,1,0:T(4,128)(2,1)S(1)} %get-tuple-element.90), channel_id=1, source_target_pairs={{16,0},{32,16},{48,32},{64,48},{80,64},{96,80},{112,96},{128,112},... | collective-permute-start | bytes 155528 | tf_op jit(solution)/shard_map/ppermute | solution.py:253
  41.2 13.8 %copy-start.10 = (f32[1,1,192]{2,1,0:T(1,128)}, f32[1,1,192]{2,1,0:T(1,128)S(1)}, u32[]{:S(2)}) copy-start(f32[1,1,192]{2,1,0:T(1,128)S(1)} %get-tuple-element.115) | copy-start | bytes 2308
  41.3 13.8 %copy-start.12 = (f32[1,1,192]{2,1,0:T(1,128)}, f32[1,1,192]{2,1,0:T(1,128)S(1)}, u32[]{:S(2)}) copy-start(f32[1,1,192]{2,1,0:T(1,128)S(1)} %get-tuple-element.116) | copy-start | bytes 2308
  41.3 13.8 %copy-start.14 = (f32[1,1,192]{2,1,0:T(1,128)}, f32[1,1,192]{2,1,0:T(1,128)S(1)}, u32[]{:S(2)}) copy-start(f32[1,1,192]{2,1,0:T(1,128)S(1)} %get-tuple-element.117) | copy-start | bytes 2308
  41.3 13.8 %copy-start.16 = (f32[1,1,192]{2,1,0:T(1,128)}, f32[1,1,192]{2,1,0:T(1,128)S(1)}, u32[]{:S(2)}) copy-start(f32[1,1,192]{2,1,0:T(1,128)S(1)} %get-tuple-element.118) | copy-start | bytes 2308
  41.3 13.8 %copy-start.18 = (f32[1,1,192]{2,1,0:T(1,128)}, f32[1,1,192]{2,1,0:T(1,128)S(1)}, u32[]{:S(2)}) copy-start(f32[1,1,192]{2,1,0:T(1,128)S(1)} %get-tuple-element.119) | copy-start | bytes 2308
  41.3 13.8 %copy-start.20 = (f32[1,1,192]{2,1,0:T(1,128)}, f32[1,1,192]{2,1,0:T(1,128)S(1)}, u32[]{:S(2)}) copy-start(f32[1,1,192]{2,1,0:T(1,128)S(1)} %get-tuple-element.120) | copy-start | bytes 2308
  41.3 13.8 %copy-start.22 = (f32[1,1,192]{2,1,0:T(1,128)}, f32[1,1,192]{2,1,0:T(1,128)S(1)}, u32[]{:S(2)}) copy-start(f32[1,1,192]{2,1,0:T(1,128)S(1)} %get-tuple-element.121) | copy-start | bytes 2308
  41.3 13.8 %copy-start.24 = (f32[1,1,192]{2,1,0:T(1,128)}, f32[1,1,192]{2,1,0:T(1,128)S(1)}, u32[]{:S(2)}) copy-start(f32[1,1,192]{2,1,0:T(1,128)S(1)} %get-tuple-element.122) | copy-start | bytes 2308
  41.3 13.8 %copy-start.26 = (f32[1,1,192]{2,1,0:T(1,128)}, f32[1,1,192]{2,1,0:T(1,128)S(1)}, u32[]{:S(2)}) copy-start(f32[1,1,192]{2,1,0:T(1,128)S(1)} %get-tuple-element.123) | copy-start | bytes 2308
  41.3 13.8 %copy-start.28 = (f32[1,1,192]{2,1,0:T(1,128)}, f32[1,1,192]{2,1,0:T(1,128)S(1)}, u32[]{:S(2)}) copy-start(f32[1,1,192]{2,1,0:T(1,128)S(1)} %get-tuple-element.124) | copy-start | bytes 2308
  41.3 13.8 %copy-start.30 = (f32[1,1,192]{2,1,0:T(1,128)}, f32[1,1,192]{2,1,0:T(1,128)S(1)}, u32[]{:S(2)}) copy-start(f32[1,1,192]{2,1,0:T(1,128)S(1)} %get-tuple-element.125) | copy-start | bytes 2308
  41.4 13.8 %copy-start.32 = (f32[1,1,192]{2,1,0:T(1,128)}, f32[1,1,192]{2,1,0:T(1,128)S(1)}, u32[]{:S(2)}) copy-start(f32[1,1,192]{2,1,0:T(1,128)S(1)} %get-tuple-element.126) | copy-start | bytes 2308
  41.4 13.8 %copy-start.34 = (f32[1,1,192]{2,1,0:T(1,128)}, f32[1,1,192]{2,1,0:T(1,128)S(1)}, u32[]{:S(2)}) copy-start(f32[1,1,192]{2,1,0:T(1,128)S(1)} %get-tuple-element.127) | copy-start | bytes 2308
  41.4 13.8 %copy-start.36 = (f32[1,1,192]{2,1,0:T(1,128)}, f32[1,1,192]{2,1,0:T(1,128)S(1)}, u32[]{:S(2)}) copy-start(f32[1,1,192]{2,1,0:T(1,128)S(1)} %get-tuple-element.128) | copy-start | bytes 2308
  44.4 4.7 %collective-permute-start.2 = (bf16[3,51,192]{2,1,0:T(8,128)(2,1)S(1)}, bf16[3,51,192]{2,1,0:T(8,128)(2,1)S(1)}, u32[]{:S(2)}, u32[]{:S(2)}) collective-permute-start(bf16[3,51,192]{2,1,0:T(8,128)(2,1)S(1)} %get-tuple-element.85), channel_id=1, source_target_pairs={{0,1},{1,2},{2,3},{3,4},{4,5},{5,6},{6,7},{7,8},{8,9},{9,10},{10,1... | collective-permute-start | bytes 176264 | tf_op jit(solution)/shard_map/ppermute | solution.py:250
  46.6 5.9 %collective-permute-start.3 = (bf16[3,51,192]{2,1,0:T(8,128)(2,1)S(1)}, bf16[3,51,192]{2,1,0:T(8,128)(2,1)S(1)}, u32[]{:S(2)}, u32[]{:S(2)}) collective-permute-start(bf16[3,51,192]{2,1,0:T(8,128)(2,1)S(1)} %get-tuple-element.86), channel_id=1, source_target_pairs={{1,0},{2,1},{3,2},{4,3},{5,4},{6,5},{7,6},{8,7},{9,8},{10,9},{11,1... | collective-permute-start | bytes 176264 | tf_op jit(solution)/shard_map/ppermute | solution.py:253
  73.7 14.6 %copy-start = (f32[45,45,192]{2,1,0:T(8,128)}, f32[45,45,192]{2,1,0:T(8,128)S(1)}, u32[]{:S(2)}) copy-start(f32[45,45,192]{2,1,0:T(8,128)S(1)} %get-tuple-element.77) | copy-start | bytes 4665604
  122.3 7.1 %collective-permute-start.4 = (bf16[45,3,192]{2,1,0:T(4,128)(2,1)S(1)}, bf16[45,3,192]{2,1,0:T(4,128)(2,1)S(1)}, u32[]{:S(2)}, u32[]{:S(2)}) collective-permute-start(bf16[45,3,192]{2,1,0:T(4,128)(2,1)S(1)} %copy-done.9), channel_id=1, source_target_pairs={{0,16},{16,32},{32,48},{48,64},{64,80},{80,96},{96,112},{112,128},... | collective-permute-start | bytes 155528 | tf_op jit(solution)/shard_map/ppermute | solution.py:250
  124.8 5.6 %collective-permute-start.5 = (bf16[45,3,192]{2,1,0:T(4,128)(2,1)S(1)}, bf16[45,3,192]{2,1,0:T(4,128)(2,1)S(1)}, u32[]{:S(2)}, u32[]{:S(2)}) collective-permute-start(bf16[45,3,192]{2,1,0:T(4,128)(2,1)S(1)} %copy-done.8), channel_id=1, source_target_pairs={{16,0},{32,16},{48,32},{64,48},{80,64},{96,80},{112,96},{128,112},... | collective-permute-start | bytes 155528 | tf_op jit(solution)/shard_map/ppermute | solution.py:253
  130.4 34.2 %collective-permute-start.6 = (bf16[3,51,192]{2,1,0:T(8,128)(2,1)S(1)}, bf16[3,51,192]{2,1,0:T(8,128)(2,1)S(1)}, u32[]{:S(2)}, u32[]{:S(2)}) collective-permute-start(bf16[3,51,192]{2,1,0:T(8,128)(2,1)S(1)} %get-tuple-element.81), channel_id=1, source_target_pairs={{1,0},{2,1},{3,2},{4,3},{5,4},{6,5},{7,6},{8,7},{9,8},{10,9},{11,1... | collective-permute-start | bytes 176264 | tf_op jit(solution)/shard_map/ppermute | solution.py:253
  132.3 32.2 %collective-permute-start.7 = (bf16[3,51,192]{2,1,0:T(8,128)(2,1)S(1)}, bf16[3,51,192]{2,1,0:T(8,128)(2,1)S(1)}, u32[]{:S(2)}, u32[]{:S(2)}) collective-permute-start(bf16[3,51,192]{2,1,0:T(8,128)(2,1)S(1)} %get-tuple-element.82), channel_id=1, source_target_pairs={{0,1},{1,2},{2,3},{3,4},{4,5},{5,6},{6,7},{7,8},{8,9},{9,10},{10,1... | collective-permute-start | bytes 176264 | tf_op jit(solution)/shard_map/ppermute | solution.py:250
  (76 other events, 473.2 us)

commit v2 on v0

v2 whole, which is shorter than its diff:
```python
import functools
import math

import jax
import jax.numpy as jnp
from jax import lax
from jax.experimental import pallas as pl
from jax.experimental.pallas import tpu as pltpu
from jax.sharding import PartitionSpec as P

C = 192
H = 768
KS = 7
EPSILON = 1e-06
STEP_SIZE = 0.003
NOISE_COEF = 0.08
ROOT = math.sqrt(2.0 / math.pi)
CUBIC = 0.044715

MESH = pl.DeviceIdType.MESH
F32 = jnp.float32
BF16 = jnp.bfloat16
SHARD = 1200
NLAT = 16
NLON = 16
GROUP_ROWS = NLAT * SHARD // 128
HALF_ROWS = GROUP_ROWS // 2
SLOT = 80
FLAT_ROWS = 2416
OUT_ROW = C * H // 128
SMALL_ROW = 2 * C * H // 128
BIAS_IN_ROW = SMALL_ROW + 52 * C // 128
SMALL = 58
HALF_SMALL = SMALL // 2

SIDE = 45
PITCH = SIDE + KS - 1
STRIP = 6
XROWS = 2760
CELLS = SIDE * SIDE
FLAT_CELLS = 8 * STRIP * SIDE
BLOCK = 512
HALF_COLS = 22

EDGES = ((-1, 0), (1, 0), (0, -1), (0, 1))
CORNERS = ((-1, -1), (-1, 1), (1, -1), (1, 1))


def first_row(k):
    return k * SHARD // 128


def small_row(r):
    return (r % 2) * HALF_SMALL + r // 2


def low_lanes(rows):
    return lax.broadcasted_iota(jnp.int32, (rows, 128), 1) < 64


def wrapped(name, size, step):
    return lax.rem(lax.axis_index(name) + step + size, size)


def remote(source, target, send_sem, recv_sem, device):
    return pltpu.make_async_remote_copy(
        src_ref=source,
        dst_ref=target,
        send_sem=send_sem,
        recv_sem=recv_sem,
        device_id=device,
        device_id_type=MESH,
    )


def signal_all():
    barrier = pltpu.get_barrier_semaphore()
    devices = [{"lat": wrapped("lat", NLAT, d)} for d in range(1, NLAT)]
    devices += [{"lon": wrapped("lon", NLON, d)} for d in range(1, NLON)]
    devices += [
        {"lat": wrapped("lat", NLAT, a), "lon": wrapped("lon", NLON, b)} for a, b in CORNERS
    ]
    for device in devices:
        pl.semaphore_signal(barrier, inc=1, device_id=device, device_id_type=MESH)
    return barrier, len(devices)


def halo_copies(edge, corner, edge_in, corner_in, send_sem, recv_sem):
    copies = []
    for q, (a, b) in enumerate(EDGES + CORNERS):
        device = {"lat": wrapped("lat", NLAT, a), "lon": wrapped("lon", NLON, b)}
        source, target = (edge, edge_in) if q < 4 else (corner, corner_in)
        slot = q % 4
        copies.append(
            remote(source.at[slot], target.at[slot], send_sem.at[q], recv_sem.at[q], device)
        )
    return copies


def pack_halo(x, edge, corner):
    for t in range(2):
        lanes = pl.ds(128 * t, 128)
        for n in range(3):
            for q, start in enumerate((3, 45)):
                edge[q, n, :, lanes] = x[t, pl.ds((start + n) * PITCH + 3, 48), :].astype(BF16)
            for q, start in enumerate((3, 45)):
                edge[2 + q, n, :, lanes] = x[
                    t, pl.ds(3 * PITCH + start + n, 48, stride=PITCH), :
                ].astype(BF16)
            for q, (a, b) in enumerate(CORNERS):
                row = 3 if a < 0 else 45
                col = 3 if b < 0 else 45
                corner[q, n, :, lanes] = x[t, pl.ds((row + n) * PITCH + col, 16), :].astype(BF16)


def unpack_halo(x, edge_in, corner_in):
    lat = lax.axis_index("lat")
    keep_top = jnp.where(lat > 0, 1.0, 0.0).astype(F32)
    keep_bottom = jnp.where(lat < NLAT - 1, 1.0, 0.0).astype(F32)
    for t in range(2):
        lanes = pl.ds(128 * t, 128)
        for n in range(3):
            for q, (row, keep) in enumerate(((48, keep_bottom), (0, keep_top))):
                x[t, pl.ds((row + n) * PITCH + 3, SIDE), :] = (
                    edge_in[q, n, :, lanes].astype(F32)[:SIDE] * keep
                )
            for q, col in enumerate((48, 0)):
                x[t, pl.ds(3 * PITCH + col + n, SIDE, stride=PITCH), :] = edge_in[
                    2 + q, n, :, lanes
                ].astype(F32)[:SIDE]
            for q, (a, b) in enumerate(CORNERS):
                row, keep = (48, keep_bottom) if a < 0 else (0, keep_top)
                col = 48 if b < 0 else 0
                x[t, pl.ds((row + n) * PITCH + col, 3), :] = (
                    corner_in[q, n, :, lanes].astype(F32)[:3] * keep
                )


def clear(ref, rows):
    for t in range(2):
        ref[t] = jnp.zeros((rows, 128), F32)


def pair_columns(ref, rows):
    def step(n, _):
        here = pl.ds(pl.multiple_of(n * 40, 8), 40)
        ahead = ref[1, pl.ds(n * 40 + HALF_COLS, 40), :]
        ref[1, here, :] = jnp.where(low_lanes(40), ref[1, here, :], pltpu.roll(ahead, 64, 1))
        return 0

    lax.fori_loop(0, rows // 40, step, 0)


def conv_tile(x, w, t, flip, bias_row, emit):
    def step(jj, _):
        j = jj * 3
        if t == 1:
            j = jnp.minimum(j, HALF_COLS - 2)
        if bias_row is None:
            start = jnp.zeros((8, 128), F32)
        else:
            start = w[t, pl.ds(bias_row, 8, stride=0), :]
        accs = [[start] * STRIP for _ in range(3)]
        for b in range(KS):
            ws = []
            for a in range(KS):
                r = (KS - 1 - a) * KS + KS - 1 - b if flip else a * KS + b
                ws.append(w[t, pl.ds(small_row(r), 8, stride=0), :])
            for c in range(3):
                for rr in range(STRIP + KS - 1):
                    v = x[t, pl.ds(rr * PITCH + j + b + c, 8, stride=STRIP * PITCH), :]
                    for a in range(KS):
                        if 0 <= rr - a < STRIP:
                            accs[c][rr - a] = accs[c][rr - a] + ws[a] * v
        for c in range(3):
            for r in range(STRIP):
                emit(r, j + c, accs[c][r])
        return 0

    lax.fori_loop(0, 15 if t == 0 else 8, step, 0)


def column_slice(r, j):
    return pl.ds(r * SIDE + j, 8, stride=STRIP * SIDE)


def emit_into(out, t):
    def emit(r, j, value):
        if t == 0:
            out[0, column_slice(r, j), :] = value
        else:
            low = low_lanes(8)
            out[1, column_slice(r, j), :] = jnp.where(low, value, 0.0)
            out[1, column_slice(r, j + HALF_COLS), :] = jnp.where(
                low, pltpu.roll(value, 64, 1), 0.0
            )

    return emit


def kernel_grad_tile(x, g, t, gk):
    count = SIDE if t == 0 else HALF_COLS + 1

    def per_col(b, _):
        def step(j, accs):
            accs = list(accs)
            gs = [g[t, column_slice(r, j), :] for r in range(STRIP)]
            for rr in range(STRIP + KS - 1):
                v = x[t, pl.ds(rr * PITCH + j + b, 8, stride=STRIP * PITCH), :]
                for a in range(KS):
                    if 0 <= rr - a < STRIP:
                        accs[a] = accs[a] + gs[rr - a] * v
            return tuple(accs)

        accs = tuple(jnp.zeros((8, 128), F32) for _ in range(KS))
        start = 0
        if t == 1:
            accs = step(0, accs)
            accs = step(1, accs)
            start = 2
        accs = lax.fori_loop(0, (count - start) // 3, lambda n, s: step3(n, s, step, start), accs)
        for a in range(KS):
            total = jnp.sum(accs[a], axis=0, keepdims=True)
            if t == 1:
                total = total + pltpu.roll(total, 64, 1)
            gk[t, pl.ds(b * 8 + a, 1), :] = total
        return 0

    lax.fori_loop(0, KS, per_col, 0)


def step3(n, accs, step, start):
    for c in range(3):
        accs = step(3 * n + c + start, accs)
    return accs


def step_kernel(
    feat_hbm, up_hbm, p_ref, noise_ref, out_hbm, fgrad_hbm, new_ref,
    feat, ups, outb, fgb, x, gp, o, gf, uf,
    win, wout, wide, ws, wz, flat,
    nrm, std, inv, pre, gact, act, gpre, gb, gwin, gwt, sg, gk, sums,
    pad_p, pad_n, send1, s1, s2, group,
    sh, xr, sb, r1, send3, r3,
    edge, corner, edge_in, corner_in, edge2, corner2, edge2_in, corner2_in,
    io_sem, ss1, rs1, ss2, rs2, fs, fr, hs, hr, hs2, hr2, xs, xrs, ls, lr, ss3, rs3,
):
    lat = lax.axis_index("lat")
    lon = lax.axis_index("lon")
    core = lax.rem(lat, 2)
    chip = lax.div(lat, 2)
    half = lax.div(lat, 8)
    place = lax.rem(lat, 8)
    partner = {"lat": lat + 1 - 2 * core}

    feat_copy = pltpu.make_async_copy(feat_hbm, feat, io_sem.at[0])
    up_copy = pltpu.make_async_copy(up_hbm, ups, io_sem.at[1])
    feat_copy.start()
    up_copy.start()
    barrier, count = signal_all()

    for ref, padded in ((p_ref, pad_p), (noise_ref, pad_n)):
        padded[...] = jnp.zeros((16, 128), F32)
        for r in range(9):
            padded[r, :] = ref[pl.ds(128 * r, 128)]
        padded[9, 0:48] = ref[pl.ds(1152, 48)]
    off = lax.rem(lat * (SHARD % 128), 128)
    lane = lax.broadcasted_iota(jnp.int32, (16, 128), 1)
    rolled = pltpu.roll(pad_p[...], off, 1)
    block = jnp.where(lane < off, pltpu.roll(rolled, 1, 0), rolled).astype(BF16)
    send1[...] = block
    pl.semaphore_wait(barrier, count)

    shard_copies = []
    for q in range(8):
        peer = 2 * q + half
        copy = remote(send1, s1.at[place], ss1.at[q], rs1.at[place], {"lat": peer})
        shard_copies.append((peer, copy))
        pl.when(peer != lat)(copy.start)

    @pl.when(half == core)
    def _():
        s1[place] = block

    clear(x, XROWS)
    feat_copy.wait()

    def load_row(i, _):
        row = feat[i].astype(F32)
        x[0, pl.ds((i + 3) * PITCH + 3, SIDE), :] = row[:, :128]
        x[1, pl.ds((i + 3) * PITCH + 3, SIDE), 0:64] = row[:, 128:]
        return 0

    lax.fori_loop(0, SIDE, load_row, 0)
    pack_halo(x, edge, corner)
    halo = halo_copies(edge, corner, edge_in, corner_in, hs, hr)
    for copy in halo:
        copy.start()

    group[...] = jnp.zeros((88, 128), F32)
    for m in range(8):
        source = 8 * core + m
        pl.when(source != lat)(
            remote(send1, s1.at[m], ss1.at[m], rs1.at[m], {"lat": lat}).wait_recv
        )
    for m in range(8):
        rows = pl.ds(first_row(m), 16)
        group[rows, :] = group[rows, :] + s1[m].astype(F32)
    s2[core, lon] = group[0:SLOT, :].astype(BF16)
    for peer, copy in shard_copies:
        pl.when(peer != lat)(copy.wait_send)
    spread = []
    for d in range(1, NLON):
        copy = remote(
            s2.at[core, lon], s2.at[core, lon], ss2.at[d], rs2.at[lon], {"lon": wrapped("lon", NLON, d)}
        )
        copy.start()
        spread.append(copy)

    clear(uf, FLAT_CELLS)
    up_copy.wait()

    def load_up(i, _):
        row = ups[i].astype(F32)
        uf[0, pl.ds(i * SIDE, SIDE), :] = row[:, :128]
        uf[1, pl.ds(i * SIDE, SIDE), 0:64] = row[:, 128:]
        return 0

    lax.fori_loop(0, SIDE, load_up, 0)
    clear(gp, XROWS)
    gwin[...] = jnp.zeros((256, H), F32)
    gwt[...] = jnp.zeros((256, H), F32)
    sums[...] = jnp.zeros((2, 64, 128), F32)
    for copy in halo:
        copy.wait()
    unpack_halo(x, edge_in, corner_in)
    pair_columns(x, 2720)

    def forward(s):
        pl.when(lon != s)(
            remote(s2.at[core, s], s2.at[core, s], ss2.at[0], rs2.at[s], {"lon": lon}).wait_recv
        )
        copy = remote(s2.at[core, s], s2.at[core, s], fs.at[s], fr.at[s], partner)
        copy.start()
        return copy

    def place_group(s):
        for h in range(2):
            flat[pl.ds(s * GROUP_ROWS + h * HALF_ROWS, SLOT), :] = s2[h, s].astype(F32)

    last = forward(NLON - 1)
    last.wait_send()
    remote(s2.at[1 - core, NLON - 1], s2.at[1 - core, NLON - 1], fs.at[NLON - 1], fr.at[NLON - 1], partner).wait_recv()
    place_group(NLON - 1)
    for t, small in enumerate(unpack_pairs(flat, SMALL_ROW, HALF_SMALL)):
        for parity in range(2):
            value = small[parity]
            if t == 1:
                low = low_lanes(HALF_SMALL)
                wz[1, parity * HALF_SMALL : (parity + 1) * HALF_SMALL, :] = jnp.where(low, value, 0.0)
                value = jnp.where(low, value, pltpu.roll(value, 64, 1))
            else:
                wz[0, parity * HALF_SMALL : (parity + 1) * HALF_SMALL, :] = value
            ws[t, parity * HALF_SMALL : (parity + 1) * HALF_SMALL, :] = value

    bias_row = small_row(49)
    conv_tile(x, ws, 0, False, bias_row, emit_into(o, 0))
    passed = [forward(s) for s in range(NLON - 1)]
    conv_tile(x, ws, 1, False, bias_row, emit_into(o, 1))
    for s, copy in enumerate(passed):
        copy.wait_send()
        remote(s2.at[1 - core, s], s2.at[1 - core, s], fs.at[s], fr.at[s], partner).wait_recv()
    for copy in spread:
        copy.wait_send()
    for s in range(NLON):
        place_group(s)

    win[192:256, :] = jnp.zeros((64, H), BF16)
    first = lax.broadcasted_iota(jnp.int32, (16, 128), 0) == 0
    for j in range(H // 128):
        lanes = pl.ds(128 * j, 128)
        win[0:C, lanes] = flat[pl.ds(j, C, stride=H // 128), :].astype(BF16)
        bias = flat[pl.ds(BIAS_IN_ROW + j, 16, stride=0), :]
        win[192:208, lanes] = jnp.where(first, bias, 0.0).astype(BF16)
    for t, values in enumerate(unpack_pairs(flat, OUT_ROW, H // 2)):
        for parity in range(2):
            wide[t, pl.ds(parity, H // 2, stride=2), :] = values[parity]
    wout[:, 0:128] = wide[0].astype(BF16)
    wout[:, 128:256] = jnp.where(low_lanes(H), wide[1], 0.0).astype(BF16)

    gain = [wz[t, small_row(50) : small_row(50) + 1, :] for t in range(2)]
    shift = [wz[t, small_row(51) : small_row(51) + 1, :] for t in range(2)]
    bias_out = [wz[t, small_row(56) : small_row(56) + 1, :] for t in range(2)]
    scale = [wz[t, small_row(57) : small_row(57) + 1, :] for t in range(2)]

    def mean(values):
        return jnp.sum(values[0] + values[1], axis=1, keepdims=True) * (1.0 / C)

    def fold(value):
        return jnp.sum(value.reshape(-1, 8, 128), axis=0)

    def mlp_block(n, _):
        base = n * BLOCK

        def norm_strip(s, _):
            rows = pl.ds(pl.multiple_of(base + s * 64, 64), 64)
            local = pl.ds(pl.multiple_of(s * 64, 64), 64)
            low = low_lanes(64)
            conv = [o[t, rows, :] for t in range(2)]
            m = mean(conv)
            centred = [conv[0] - m, jnp.where(low, conv[1] - m, 0.0)]
            inverse = lax.rsqrt(mean([v * v for v in centred]) + EPSILON)
            inv[local, :] = jnp.broadcast_to(inverse, (64, 128))
            for t in range(2):
                standard = centred[t] * inverse
                std[t, local, :] = standard
                value = standard * gain[t] + shift[t]
                if t == 1:
                    ones = lax.broadcasted_iota(jnp.int32, (64, 128), 1) == 64
                    value = jnp.where(ones, 1.0, value)
                nrm[local, 128 * t : 128 * t + 128] = value.astype(BF16)
                gb[local, 128 * t : 128 * t + 128] = (scale[t] * uf[t, rows, :]).astype(BF16)
            return 0

        lax.fori_loop(0, BLOCK // 64, norm_strip, 0)
        pre[...] = jnp.dot(nrm[...], win[...], preferred_element_type=F32)
        gact[...] = lax.dot_general(
            gb[...], wout[...], (((1,), (1,)), ((), ())), preferred_element_type=F32
        )

        def gelu_strip(s, _):
            local = pl.ds(pl.multiple_of(s * 16, 16), 16)
            for j in range(2):
                lanes = pl.ds(384 * j, 384)
                v = pre[local, lanes]
                square = v * v
                t = jnp.tanh(v * (ROOT + (ROOT * CUBIC) * square))
                hv = 0.5 * v
                act[local, lanes] = (hv + hv * t).astype(BF16)
                slope = 0.5 + 0.5 * t + hv * (1.0 - t * t) * (ROOT + (3.0 * ROOT * CUBIC) * square)
                gpre[local, lanes] = (gact[local, lanes] * slope).astype(BF16)
            return 0

        lax.fori_loop(0, BLOCK // 16, gelu_strip, 0)
        pre[:, 0:256] = jnp.dot(act[...], wout[...], preferred_element_type=F32)
        pre[:, 256:512] = lax.dot_general(
            gpre[...], win[...], (((1,), (1,)), ((), ())), preferred_element_type=F32
        )
        gwin[...] += lax.dot_general(
            nrm[...], gpre[...], (((0,), (0,)), ((), ())), preferred_element_type=F32
        )
        gwt[...] += lax.dot_general(
            gb[...], act[...], (((0,), (0,)), ((), ())), preferred_element_type=F32
        )

        def back_strip(s, totals):
            rows = pl.ds(pl.multiple_of(base + s * 64, 64), 64)
            local = pl.ds(pl.multiple_of(s * 64, 64), 64)
            totals = list(totals)
            low = low_lanes(64)
            scaled, standard = [], []
            for t in range(2):
                branch = pre[local, 128 * t : 128 * t + 128] + bias_out[t]
                o[t, rows, :] = scale[t] * branch
                st = std[t, local, :]
                gn = pre[local, 256 + 128 * t : 384 + 128 * t]
                totals[4 * t] += fold(gn * st)
                totals[4 * t + 1] += fold(gn)
                totals[4 * t + 2] += fold(gb[local, 128 * t : 128 * t + 128].astype(F32))
                totals[4 * t + 3] += fold(branch * uf[t, rows, :])
                scaled.append(gn * gain[t])
                standard.append(st)
            m1 = mean(scaled)
            m2 = mean([a * b for a, b in zip(scaled, standard)])
            inverse = inv[local, :]
            for t in range(2):
                g = ((scaled[t] - m1 - standard[t] * m2) * inverse).astype(BF16).astype(F32)
                gf[t, rows, :] = g if t == 0 else jnp.where(low, g, 0.0)
            return tuple(totals)

        zeros = tuple(jnp.zeros((8, 128), F32) for _ in range(8))
        totals = lax.fori_loop(0, BLOCK // 64, back_strip, zeros)
        for k in range(8):
            rows = pl.ds(8 * (k % 4), 8)
            sums[k // 4, rows, :] = sums[k // 4, rows, :] + totals[k]
        return 0

    lax.fori_loop(0, 4, mlp_block, 0)
    for t in range(2):
        gf[t, 2048:FLAT_CELLS, :] = jnp.zeros((FLAT_CELLS - 2048, 128), F32)

    def grad_row(i, _):
        for t in range(2):
            gp[t, pl.ds((i + 3) * PITCH + 3, SIDE), :] = gf[t, pl.ds(i * SIDE, SIDE), :]
        return 0

    lax.fori_loop(0, SIDE, grad_row, 0)
    pack_halo(gp, edge2, corner2)
    halo2 = halo_copies(edge2, corner2, edge2_in, corner2_in, hs2, hr2)
    for copy in halo2:
        copy.start()

    for j in range(H // 128):
        flat[pl.ds(j, C, stride=H // 128), :] = gwin[0:C, 128 * j : 128 * j + 128]
    wide[0] = jnp.transpose(gwt[0:128, :])
    wide[1] = jnp.transpose(gwt[128:256, :])
    pack_pairs(
        flat, OUT_ROW, H // 2,
        [[wide[t, pl.ds(parity, H // 2, stride=2), :] for parity in range(2)] for t in range(2)],
    )

    def stage_half(l):
        for h in range(2):
            sh[h, l] = flat[pl.ds(l * GROUP_ROWS + h * HALF_ROWS, SLOT), :].astype(BF16)

    for l in range(NLON - 1):
        stage_half(l)
    bulk = remote(
        sh.at[1 - core, pl.ds(0, NLON - 1)], xr.at[pl.ds(0, NLON - 1)], xs.at[0], xrs.at[0], partner
    )
    bulk.start()

    def out_row(i, _):
        row = feat[i].astype(F32)
        rows = pl.ds(i * SIDE, SIDE)
        outb[i, :, 0:128] = (row[:, :128] + o[0, rows, :]).astype(BF16)
        outb[i, :, 128:192] = (row[:, 128:] + o[1, rows, :][:, :64]).astype(BF16)
        return 0

    lax.fori_loop(0, SIDE, out_row, 0)
    out_copy = pltpu.make_async_copy(outb, out_hbm, io_sem.at[2])
    out_copy.start()

    for t in range(2):
        total = jnp.sum(gf[t].reshape(-1, 8, 128), axis=0)
        sums[t, 32:40, :] = total
    pair_columns(gf, 2120)
    column = gf[1, pl.ds(0, SIDE, stride=SIDE), :]
    gf[1, pl.ds(0, SIDE, stride=SIDE), :] = jnp.where(low_lanes(SIDE), column, 0.0)

    kernel_grad_tile(x, gf, 0, gk)
    bulk.wait()

    def add_half(l):
        return (sh[core, l].astype(F32) + xr[l].astype(F32)).astype(BF16)

    for l in range(NLON - 1):
        sb[l] = add_half(l)
    blocks = []
    for l in range(NLON):
        blocks.append(remote(sb.at[l], r1.at[lon], ls.at[l], lr.at[lon], {"lon": l}))
    for l in range(NLON - 1):
        pl.when(lon != l)(blocks[l].start)

        @pl.when(lon == l)
        def _():
            r1[l] = sb[l]

    kernel_grad_tile(x, gf, 1, gk)

    for t in range(2):
        for r in range(KS * KS):
            sg[t, small_row(r), :] = gk[t, (r % KS) * 8 + r // KS, :]
        for r, k in ((49, 4), (50, 0), (51, 1), (56, 2), (57, 3)):
            sg[t, small_row(r), :] = jnp.sum(sums[t, 8 * k : 8 * k + 8, :], axis=0)
        for r in range(52, 56):
            sg[t, small_row(r), :] = jnp.zeros((128,), F32)
    flat[pl.ds(SMALL_ROW + 80, FLAT_ROWS - SMALL_ROW - 80), :] = jnp.zeros(
        (FLAT_ROWS - SMALL_ROW - 80, 128), F32
    )
    pack_pairs(
        flat, SMALL_ROW, HALF_SMALL,
        [
            [sg[t, parity * HALF_SMALL : (parity + 1) * HALF_SMALL, :] for parity in range(2)]
            for t in range(2)
        ],
    )
    for j in range(H // 128):
        flat[BIAS_IN_ROW + j, :] = gwin[192, 128 * j : 128 * j + 128]
    stage_half(NLON - 1)
    tail = remote(sh.at[1 - core, NLON - 1], xr.at[NLON - 1], xs.at[1], xrs.at[1], partner)
    tail.start()

    for copy in halo2:
        copy.wait()
    unpack_halo(gp, edge2_in, corner2_in)
    pair_columns(gp, 2720)
    tail.wait()
    sb[NLON - 1] = add_half(NLON - 1)
    pl.when(lon != NLON - 1)(blocks[NLON - 1].start)

    @pl.when(lon == NLON - 1)
    def _():
        r1[NLON - 1] = sb[NLON - 1]

    conv_tile(gp, ws, 0, True, None, emit_into(o, 0))
    conv_tile(gp, ws, 1, True, None, emit_into(o, 1))

    def grad_out_row(i, _):
        row = ups[i].astype(F32)
        rows = pl.ds(i * SIDE, SIDE)
        fgb[i, :, 0:128] = (row[:, :128] + o[0, rows, :]).astype(BF16)
        fgb[i, :, 128:192] = (row[:, 128:] + o[1, rows, :][:, :64]).astype(BF16)
        return 0

    lax.fori_loop(0, SIDE, grad_out_row, 0)
    fgrad_copy = pltpu.make_async_copy(fgb, fgrad_hbm, io_sem.at[3])
    fgrad_copy.start()

    for s in range(NLON):
        pl.when(lon != s)(remote(sb.at[s], r1.at[s], ls.at[s], lr.at[s], {"lon": lon}).wait_recv)
    total = r1[0].astype(F32)
    for s in range(1, NLON):
        total = total + r1[s].astype(F32)
    group[0:SLOT, :] = total
    for m in range(8):
        send3[m] = group[pl.ds(first_row(m), 16), :]
    pieces = []
    for m in range(8):
        owner = 8 * core + m
        copy = remote(send3.at[m], r3.at[chip], ss3.at[m], rs3.at[chip], {"lat": owner})
        pieces.append((owner, copy))
        pl.when(owner != lat)(copy.start)

    @pl.when(half == core)
    def _():
        r3[chip] = send3[place]

    for q in range(8):
        source = 2 * q + half
        pl.when(source != lat)(
            remote(send3.at[q], r3.at[q], ss3.at[q], rs3.at[q], {"lat": lat}).wait_recv
        )
    total = r3[0]
    for q in range(1, 8):
        total = total + r3[q]
    mixed = jnp.where(lane < off, pltpu.roll(total, 15, 0), total)
    grads = pltpu.roll(mixed, lax.rem(128 - off, 128), 1)
    pad_p[...] = pad_p[...] - STEP_SIZE * grads + NOISE_COEF * pad_n[...]
    for r in range(9):
        new_ref[pl.ds(128 * r, 128)] = pad_p[r, :]
    new_ref[pl.ds(1152, 48)] = pad_p[9, 0:48]
    for l in range(NLON):
        pl.when(lon != l)(blocks[l].wait_send)
    for owner, copy in pieces:
        pl.when(owner != lat)(copy.wait_send)
    out_copy.wait()
    fgrad_copy.wait()


def unpack_pairs(flat, base, pairs):
    first = flat[pl.ds(base, pairs, stride=3), :]
    middle = flat[pl.ds(base + 1, pairs, stride=3), :]
    last = flat[pl.ds(base + 2, pairs, stride=3), :]
    last_turned = pltpu.roll(last, 64, 1)
    odd = jnp.where(low_lanes(pairs), pltpu.roll(middle, 64, 1), last_turned)
    return [[first, odd], [middle, last_turned]]


def pack_pairs(flat, base, pairs, values):
    low = low_lanes(pairs)
    odd_turned = pltpu.roll(values[0][1], 64, 1)
    tail_turned = pltpu.roll(values[1][1], 64, 1)
    flat[pl.ds(base, pairs, stride=3), :] = values[0][0]
    flat[pl.ds(base + 1, pairs, stride=3), :] = jnp.where(low, values[1][0], odd_turned)
    flat[pl.ds(base + 2, pairs, stride=3), :] = jnp.where(low, odd_turned, tail_turned)


VM = pl.BlockSpec(memory_space=pltpu.VMEM)
ANY = pl.BlockSpec(memory_space=pl.ANY)


def vm(*shape, kind=F32):
    return pltpu.VMEM(shape, kind)


def dma(n):
    return pltpu.SemaphoreType.DMA((n,))


def body(features, params, langevin_noise, upstream):
    field = features.shape
    halo_shapes = [
        vm(4, 3, 48, 256, kind=BF16), vm(4, 3, 16, 256, kind=BF16),
        vm(4, 3, 48, 256, kind=BF16), vm(4, 3, 16, 256, kind=BF16),
    ]
    return pl.pallas_call(
        step_kernel,
        out_shape=(
            jax.ShapeDtypeStruct(field, BF16),
            jax.ShapeDtypeStruct(field, BF16),
            jax.ShapeDtypeStruct(params.shape, F32),
        ),
        in_specs=[ANY, ANY, VM, VM],
        out_specs=(ANY, ANY, VM),
        scratch_shapes=[
            vm(*field, kind=BF16), vm(*field, kind=BF16), vm(*field, kind=BF16), vm(*field, kind=BF16),
            vm(2, XROWS, 128), vm(2, XROWS, 128),
            vm(2, FLAT_CELLS, 128), vm(2, FLAT_CELLS, 128), vm(2, FLAT_CELLS, 128),
            vm(256, H, kind=BF16), vm(H, 256, kind=BF16), vm(2, H, 128),
            vm(2, 64, 128), vm(2, 64, 128), vm(FLAT_ROWS, 128),
            vm(BLOCK, 256, kind=BF16), vm(2, BLOCK, 128), vm(BLOCK, 128),
            vm(BLOCK, H), vm(BLOCK, H), vm(BLOCK, H, kind=BF16), vm(BLOCK, H, kind=BF16),
            vm(BLOCK, 256, kind=BF16), vm(256, H), vm(256, H), vm(2, 64, 128), vm(2, 64, 128),
            vm(2, 64, 128),
            vm(16, 128), vm(16, 128), vm(16, 128, kind=BF16), vm(8, 16, 128, kind=BF16),
            vm(2, NLON, SLOT, 128, kind=BF16), vm(88, 128),
            vm(2, NLON, SLOT, 128, kind=BF16), vm(NLON, SLOT, 128, kind=BF16),
            vm(NLON, SLOT, 128, kind=BF16), vm(NLON, SLOT, 128, kind=BF16),
            vm(8, 16, 128), vm(8, 16, 128),
            *halo_shapes, *halo_shapes,
            dma(4), dma(8), dma(8), dma(NLON), dma(NLON), dma(NLON), dma(NLON),
            dma(8), dma(8), dma(8), dma(8), dma(2), dma(2), dma(NLON), dma(NLON), dma(8), dma(8),
        ],
        compiler_params=pltpu.CompilerParams(
            collective_id=0, has_side_effects=True, vmem_limit_bytes=60 * 1024 * 1024
        ),
        name="langevin_step",
    )(features, upstream, params, langevin_noise)


def solution(mesh):
    return jax.shard_map(
        body,
        mesh=mesh,
        in_specs=(
            P("lat", "lon", None),
            P(("lon", "lat")),
            P(("lon", "lat")),
            P("lat", "lon", None),
        ),
        out_specs=(P("lat", "lon", None), P("lat", "lon", None), P(("lon", "lat"))),
        check_vma=False,
    )
```

time: 623 us -> 95.6 us (0.15)
  waiting for transfers between devices: 477 us -> 0 us
  Pallas kernels: 0 us -> 90.8 us
  other arithmetic: 70.7 us -> 0 us
  starting transfers between devices: 26.8 us -> 0 us
  matrix products: 20.1 us -> 0 us
  between operations: 16.1 us -> 0.65 us
    unnamed x4 -> x0, waiting for transfers between devices: 473 us -> none
    pallas_call x0 -> x1, Pallas kernels: none -> 90.8 us  [body(): pl.pallas_call(step_kernel, out_shape=(jax.ShapeDtypeStruct(field, BF16),...]
    reduce_sum x6 -> x0, other arithmetic: 42 us -> none  [the longest x4 20.7 us: kernel_grad(): jnp.sum(grad_conv.astype(jnp.float32) * window.astype(jnp.float32), axis=...]
    ppermute x8 -> x0, starting transfers between devices: 26.8 us -> none  [the longest x4 13.7 us: padded_2(): lax.ppermute(lax.slice_in_dim(block, 0, width, axis=dim), axis, backward)]
    convert_element_type x5 -> x0, other arithmetic: 22.9 us -> none  [the longest x1 19.3 us: body(): field_grad = (upstream.astype(jnp.float32) + transposed(grad_padded, kern...]
    dot_general x6 -> x0, matrix products: 20.1 us -> none  [the longest x1 6.16 us: layer_pass(): jnp.einsum('ijc,hc->ijh', grad_branch, w_out, preferred_element_type=jnp....]
  transfers between devices with their start and end apart: 10 -> 0, of which waited for: 4 -> 0; matrix products, arithmetic and copies ran while one was open for 6% -> 0% of each run, Pallas kernels for 0% -> 0%
where the time goes in v2:
time: 95.6 us; the launch traced here: 95.4 us
  Pallas kernels  90.8 us (95%)
  local copies, waits for them, and re-layouts  3.99 us (4%)
    pallas_call x1, Pallas kernels, body(): pl.pallas_call(step_kernel, out_shape=(jax.ShapeDtypeStruct(field, BF16),...  90.8 us
    unnamed x7, local copies, waits for them, and re-layouts  3.99 us

profile of v2, /device:TPU:1, one launch (start us, length us, event | category | flops | bytes accessed | tf_op | source)
XLA Modules:
  0.0 95.4 jit_solution(8631618036804371434)
XLA Ops:
  0.6 90.8 %langevin_step.1 = (bf16[45,45,192]{2,1,0:T(8,128)(2,1)}, bf16[45,45,192]{2,1,0:T(8,128)(2,1)}, f32[1200]{0:T(1024)}) custom-call(bf16[45,45,192]{2,1,0:T(8,128)(2,1)} %feat_hbm.1, bf16[45,45,192]{2,1,0:T(8,128)(2,1)} %up_hbm.1, f32[1200]{0:T(1024)} %p_ref.1, f32[1200]{0:T(1024)} %noise_ref.1), custom_call_target="tpu_custom_call" | custom-call | tf_op jit(solution)/shard_map/langevin_step/pallas_call | solution.py:687
  91.4 0.0 copy-start
  91.4 2.4 %copy.10 = bf16[45,45,192]{2,1,0:T(8,128)(2,1)} copy(bf16[45,45,192]{2,1,0:T(8,128)(2,1)} %get-tuple-element.6) | data formatting | bytes 1555200
  93.8 0.0 copy-done
  93.8 0.0 copy-start.1
  93.8 1.0 %copy.11 = bf16[45,45,192]{2,1,0:T(8,128)(2,1)} copy(bf16[45,45,192]{2,1,0:T(8,128)(2,1)S(1)} %copy-done) | data formatting | bytes 1555200
  94.8 0.0 copy-done.1
  94.8 0.6 copy.12
Async XLA Ops:
  91.4 2.4 %copy-start = (bf16[45,45,192]{2,1,0:T(8,128)(2,1)S(1)}, bf16[45,45,192]{2,1,0:T(8,128)(2,1)}, u32[]{:S(2)}) copy-start(bf16[45,45,192]{2,1,0:T(8,128)(2,1)} %get-tuple-element.7) | copy-start | bytes 2332804
  93.8 1.0 %copy-start.1 = (f32[1200]{0:T(1024)S(1)}, f32[1200]{0:T(1024)}, u32[]{:S(2)}) copy-start(f32[1200]{0:T(1024)} %get-tuple-element.8) | copy-start | bytes 14404
